TPU v7x, 32 devices: a whole 2x2x4 slice. The times are simulated.
32 devices in a mesh: dp: 8 (over z, x), head: 4 (over y, core).
Axes of the slice: x: 2, y: 2, z: 4, core: 2. Of those that a mesh axis runs over, the one named last changes fastest.
Arguments:
- hidden_in: bfloat16 [8192, 2048], P(('dp', 'head')), may hold values from -6 to 6
- in_gain: float32 [2048], replicated, may hold values from 0.1 to 1.9
- gate_proj: bfloat16 [2048, 4096], P(None, 'head'), may hold values from -0.125 to 0.125
- value_proj: bfloat16 [2048, 4096], P(None, 'head'), may hold values from -0.125 to 0.125
- state_proj: bfloat16 [2048, 256], replicated, may hold values from -0.125 to 0.125
- step_proj: bfloat16 [2048, 64], P(None, 'head'), may hold values from -0.03125 to 0.03125
- conv_value: float32 [4, 4096], P(None, 'head'), may hold values from -3 to 3
- conv_value_bias: float32 [4096], P('head'), may hold values from -3 to 3
- conv_state: float32 [4, 256], replicated, may hold values from -3 to 3
- conv_state_bias: float32 [256], replicated, may hold values from -3 to 3
- step_bias: float32 [64], P('head'), may hold values from -6 to -1
- decay_log: float32 [64], P('head'), may hold values from 0 to 2.77
- skip_gain: float32 [64], P('head'), may hold values from 0.5 to 1.5
- out_gain: float32 [4096], P('head'), may hold values from 0.1 to 1.9
- out_proj: bfloat16 [4096, 2048], P('head'), may hold values from -0.125 to 0.125
- cotangent: bfloat16 [8192, 2048], P(('dp', 'head')), may hold values from -6 to 6
- width_level: int32 [8], P('dp'), may hold values from 0 to 3
Outputs:
- block_out: bfloat16 [8192, 2048], P(('dp', 'head'))
- in_grad: float32 [8192, 2048], P(('dp', 'head'))
- in_gain_grad: float32 [2048], replicated
- gate_proj_grad: float32 [2048, 4096], P('dp', 'head')
- value_proj_grad: float32 [2048, 4096], P('dp', 'head')
- state_proj_grad: float32 [2048, 256], P('dp')
- step_proj_grad: float32 [2048, 64], P('dp', 'head')
- conv_value_grad: float32 [4, 4096], P(None, 'head')
- conv_value_bias_grad: float32 [4096], P('head')
- conv_state_grad: float32 [4, 256], replicated
- conv_state_bias_grad: float32 [256], replicated
- step_bias_grad: float32 [64], P('head')
- decay_log_grad: float32 [64], P('head')
- skip_gain_grad: float32 [64], P('head')
- out_gain_grad: float32 [4096], P('head')
- out_proj_grad: float32 [4096, 2048], P('head', 'dp')
All inputs are finite; a program needn't handle non-finite values.
Results may differ from a plain program's by a relative error of at most 0.0079.
Values may be sent and summed in bfloat16 or wider, within the bound.
A program may use at most 192 MiB of HBM per device.

v0:
```python
import jax
import jax.numpy as jnp
from jax import lax
from jax.sharding import PartitionSpec as P

SPAN = 256


HIGH = lax.Precision.HIGHEST
EPS = 1e-05


def conv_causal(series, kernel, shift):
    kernel_len = kernel.shape[0]
    length = series.shape[0]
    padded = jnp.pad(series, ((kernel_len - 1, 0), (0, 0)))
    running = shift[None, :] + kernel[0][None, :] * padded[0:length]
    for offset in range(1, kernel_len):
        running = running + kernel[offset][None, :] * padded[offset : offset + length]
    return running


def state_space(inputs, step_size, decay_rate, key_rows, query_rows, skip_gain):
    seq_len, heads, head_dim = inputs.shape
    blocks = seq_len // SPAN
    values = inputs.reshape(blocks, SPAN, heads, head_dim)
    deltas = step_size.reshape(blocks, SPAN, heads)
    keys = key_rows.reshape(blocks, SPAN, -1)
    queries = query_rows.reshape(blocks, SPAN, -1)
    cumul = jnp.cumsum(deltas * decay_rate[None, None, :], axis=1)
    inner = jnp.einsum("cin,cjn->cij", queries, keys, precision=HIGH)
    lower = (jnp.arange(SPAN)[:, None] >= jnp.arange(SPAN)[None, :])[None, :, :, None]
    spread = cumul[:, :, None, :] - cumul[:, None, :, :]
    mixing = jnp.where(lower, jnp.exp(jnp.where(lower, spread, 0.0)), 0.0) * inner[:, :, :, None]
    scaled = values * deltas[:, :, :, None]
    within = jnp.einsum("cijh,cjhp->cihp", mixing, scaled, precision=HIGH)
    tails = jnp.exp(cumul[:, -1:, :] - cumul)
    states = jnp.einsum("cjhp,cjn->chpn", scaled * tails[:, :, :, None], keys, precision=HIGH)
    totals = jnp.exp(cumul[:, -1, :])

    def carry_state(state, item):
        fresh, factor = item
        return (factor[:, None, None] * state + fresh, state)

    start = jnp.zeros((heads, head_dim, keys.shape[2]), dtype=inputs.dtype)
    _, entering = lax.scan(carry_state, start, (states, totals))
    across = (
        jnp.einsum("cin,chpn->cihp", queries, entering, precision=HIGH)
        * jnp.exp(cumul)[:, :, :, None]
    )
    result = within + across + values * skip_gain[None, None, :, None]
    return result.reshape(seq_len, heads, head_dim)


def mix_block(
    value_pre,
    state_pre,
    step_pre,
    gate_pre,
    conv_value,
    conv_value_bias,
    conv_state,
    conv_state_bias,
    step_bias,
    decay_log,
    skip_gain,
    keep,
):
    seq_len = value_pre.shape[0]
    heads = step_pre.shape[1]
    value_act = jax.nn.silu(conv_causal(value_pre, conv_value, conv_value_bias))
    state_act = jax.nn.silu(conv_causal(state_pre, conv_state, conv_state_bias))
    half = state_act.shape[1] // 2
    step_size = jax.nn.softplus(step_pre + step_bias[None, :])
    inputs = value_act.reshape(seq_len, heads, -1) * keep[None, :, None]
    result = state_space(
        inputs, step_size, -jnp.exp(decay_log), state_act[:, :half], state_act[:, half:], skip_gain
    )
    return result.reshape(seq_len, -1) * jax.nn.silu(gate_pre)


def contract_rows(left, right):
    return lax.dot_general(
        left, right, (((0,), (0,)), ((), ())), preferred_element_type=jnp.float32
    )


def contract_cols(left, right):
    return lax.dot_general(
        left, right, (((1,), (1,)), ((), ())), preferred_element_type=jnp.float32
    )


def per_device(
    hidden_in,
    in_gain,
    gate_proj,
    value_proj,
    state_proj,
    step_proj,
    conv_value,
    conv_value_bias,
    conv_state,
    conv_state_bias,
    step_bias,
    decay_log,
    skip_gain,
    out_gain,
    out_proj,
    cotangent,
    width_level,
):
    heads_here = step_bias.shape[0]
    head_dim = conv_value.shape[1] // heads_here
    groups = lax.axis_size("head")
    rank = lax.axis_index("head")
    rows_own = hidden_in.shape[0]
    seqs = width_level.shape[0]
    resid = hidden_in.astype(jnp.float32)
    in_scale = lax.rsqrt(jnp.mean(resid * resid, axis=-1, keepdims=True) + EPS)
    normed = (resid * in_scale * in_gain).astype(jnp.bfloat16)
    whole = lax.all_gather(normed, "head", axis=0, tiled=True)
    rows_all = whole.shape[0]
    seq_len = rows_all // seqs
    gate_pre = jnp.dot(whole, gate_proj, preferred_element_type=jnp.float32)
    value_pre = jnp.dot(whole, value_proj, preferred_element_type=jnp.float32)
    state_pre = jnp.dot(whole, state_proj, preferred_element_type=jnp.float32)
    step_pre = jnp.dot(whole, step_proj, preferred_element_type=jnp.float32)
    active = jnp.right_shift(heads_here, 3 - width_level)
    keep = (jnp.arange(heads_here)[None, :] < active[:, None]).astype(jnp.float32)
    seq_count = (active * groups * head_dim).astype(jnp.float32)
    token_count = jnp.broadcast_to(seq_count[:, None], (seqs, seq_len)).reshape(rows_all)
    params = (
        conv_value,
        conv_value_bias,
        conv_state,
        conv_state_bias,
        step_bias,
        decay_log,
        skip_gain,
    )

    def group_mix(value_in, state_in, step_in, gate_in, *weights):

        def split(array):
            return array.reshape(seqs, seq_len, array.shape[1])

        mapped = jax.vmap(
            mix_block, in_axes=(0, 0, 0, 0, None, None, None, None, None, None, None, 0)
        )
        result = mapped(
            split(value_in), split(state_in), split(step_in), split(gate_in), *weights, keep
        )
        return result.reshape(rows_all, -1)

    gated = group_mix(value_pre, state_pre, step_pre, gate_pre, *params)
    squares = lax.psum(jnp.sum(gated * gated, axis=-1), "head")
    out_scale = lax.rsqrt(squares / token_count + EPS)[:, None]
    normed_out = (gated * out_scale * out_gain).astype(jnp.bfloat16)
    own_out = lax.psum_scatter(
        jnp.dot(normed_out, out_proj, preferred_element_type=jnp.float32),
        "head",
        scatter_dimension=0,
        tiled=True,
    )
    block_out = (resid + own_out).astype(jnp.bfloat16)
    cot_all = lax.all_gather(cotangent, "head", axis=0, tiled=True)
    out_proj_part = contract_rows(normed_out, cot_all)
    d_normed_out = contract_cols(cot_all, out_proj)
    weighted = d_normed_out * out_gain
    stat = lax.psum(jnp.sum(weighted * gated, axis=-1), "head")
    d_gated = weighted * out_scale - gated * out_scale**3 * (stat / token_count)[:, None]
    out_gain_part = jnp.sum(d_normed_out * gated * out_scale, axis=0)
    _, pull = jax.vjp(group_mix, value_pre, state_pre, step_pre, gate_pre, *params)
    (
        d_value_pre,
        d_state_pre,
        d_step_pre,
        d_gate_pre,
        g_conv_value,
        g_conv_value_bias,
        g_conv_state,
        g_conv_state_bias,
        g_step_bias,
        g_decay_log,
        g_skip_gain,
    ) = pull(d_gated)
    d_state_pre, g_conv_state, g_conv_state_bias = lax.psum(
        (d_state_pre, g_conv_state, g_conv_state_bias), "head"
    )
    d_gate_low = d_gate_pre.astype(jnp.bfloat16)
    d_value_low = d_value_pre.astype(jnp.bfloat16)
    d_state_low = d_state_pre.astype(jnp.bfloat16)
    d_step_low = d_step_pre.astype(jnp.bfloat16)
    d_normed = lax.psum_scatter(
        contract_cols(d_gate_low, gate_proj)
        + contract_cols(d_value_low, value_proj)
        + contract_cols(d_step_low, step_proj),
        "head",
        scatter_dimension=0,
        tiled=True,
    )
    state_own = lax.dynamic_slice_in_dim(d_state_low, rank * rows_own, rows_own, 0)
    d_normed = d_normed + contract_cols(state_own, state_proj)
    gate_part = contract_rows(whole, d_gate_low)
    value_part = contract_rows(whole, d_value_low)
    state_part = contract_rows(whole, d_state_low)
    step_part = contract_rows(whole, d_step_low)
    scaled_grad = d_normed * in_gain
    in_grad = (
        cotangent.astype(jnp.float32)
        + scaled_grad * in_scale
        - resid
        * in_scale**3
        * jnp.sum(scaled_grad * resid, axis=-1, keepdims=True)
        / resid.shape[1]
    )
    in_gain_grad = lax.psum(jnp.sum(d_normed * resid * in_scale, axis=0), ("dp", "head"))
    (
        conv_value_grad,
        conv_value_bias_grad,
        step_bias_grad,
        decay_log_grad,
        skip_gain_grad,
        out_gain_grad,
        conv_state_grad,
        conv_state_bias_grad,
    ) = lax.psum(
        (
            g_conv_value,
            g_conv_value_bias,
            g_step_bias,
            g_decay_log,
            g_skip_gain,
            out_gain_part,
            g_conv_state,
            g_conv_state_bias,
        ),
        "dp",
    )
    gate_proj_grad, value_proj_grad, state_proj_grad, step_proj_grad, out_proj_grad = (
        lax.psum_scatter(gate_part, "dp", scatter_dimension=0, tiled=True),
        lax.psum_scatter(value_part, "dp", scatter_dimension=0, tiled=True),
        lax.psum_scatter(state_part, "dp", scatter_dimension=0, tiled=True),
        lax.psum_scatter(step_part, "dp", scatter_dimension=0, tiled=True),
        lax.psum_scatter(out_proj_part, "dp", scatter_dimension=1, tiled=True),
    )
    return (
        block_out,
        in_grad,
        in_gain_grad,
        gate_proj_grad,
        value_proj_grad,
        state_proj_grad,
        step_proj_grad,
        conv_value_grad,
        conv_value_bias_grad,
        conv_state_grad,
        conv_state_bias_grad,
        step_bias_grad,
        decay_log_grad,
        skip_gain_grad,
        out_gain_grad,
        out_proj_grad,
    )


def solution(mesh):
    placed = (
        P(("dp", "head"), None),
        P(),
        P(None, "head"),
        P(None, "head"),
        P(),
        P(None, "head"),
        P(None, "head"),
        P("head"),
        P(),
        P(),
        P("head"),
        P("head"),
        P("head"),
        P("head"),
        P("head", None),
        P(("dp", "head"), None),
        P("dp"),
    )
    return jax.shard_map(
        per_device,
        mesh=mesh,
        in_specs=placed,
        out_specs=(
            P(("dp", "head"), None),
            P(("dp", "head"), None),
            P(),
            P("dp", "head"),
            P("dp", "head"),
            P("dp", None),
            P("dp", "head"),
            P(None, "head"),
            P("head"),
            P(),
            P(),
            P("head"),
            P("head"),
            P("head"),
            P("head"),
            P("head", "dp"),
        ),
        check_vma=False,
    )
```

profile of v0, /device:TPU:0, one launch (start us, length us, event | category | flops | bytes accessed | tf_op | source)
XLA Modules:
  0.0 1183.6 jit_solution(4698405417298480208)
XLA Ops:
  15.4 33.9 %all-gather.3.cloned.1.call-done = bf16[1024,2048]{1,0:T(8,128)(2,1)} async-done(((bf16[256,2048]{1,0:T(8,128)(2,1)}), bf16[1024,2048]{1,0:T(8,128)(2,1)}) %all-gather.3.cloned.1.call-update) | async-done | bytes 4194320 | tf_op jit(solution)/shard_map/all_gather | solution.py:122
  76.1 7.3 reshape.749
  83.4 7.2 reshape.748
  90.6 7.7 copy.284
  98.3 7.9 copy.274
  106.3 7.8 fusion.76
  114.1 20.4 %fusion.9 = f32[4,16,64,256]{3,2,1,0:T(8,128)} fusion(f32[4,256,256]{2,1,0:T(8,128)S(1)} %copy-done.20, f32[4,256,16]{1,2,0:T(8,128)S(1)} %copy-done.30, pred[256,256]{1,0:T(8,128)(4,1)S(1)} %copy-done.28, f32[4,256,16,64]{1,3,2,0:T(8,128)S(1)} %copy-done.4, f32[4,256,16]{1,2,0:T(8,128)S(1)} %bitcast.318, f32[16]{0:T(128)S(1)} %copy-done.57), kind=kOutput, calls=%fused_computation.25 | convolution fusion | flops 3240099840 | bytes 9633856 | tf_op jit(solution)/shard_map/vmap(cijh,cjhp->cihp)/dot_general | solution.py:36
  136.1 8.5 while.47
  144.6 10.0 fusion.31
  154.6 8.1 copy.324
  162.7 7.6 reshape.750
  170.3 12.6 %multiply_reduce_fusion.8 = (f32[1024]{0:T(1024)S(1)}, f32[1024,1024]{1,0:T(8,128)}, f32[1024,1024]{1,0:T(8,128)}) fusion(f32[1024,1024]{1,0:T(8,128)} %reshape.750, bf16[1024,2048]{1,0:T(8,128)(2,1)} %all-gather.3.cloned.1.call-done, bf16[2048,1024]{1,0:T(8,128)(2,1)} %param.25), kind=kOutput, calls=%fused_computation.79 | convolution fusion | flops 4302306304 | bytes 20975616 | tf_op jit(solution)/shard_map/dot_general | solution.py:125
  183.0 5.8 psum.98
  188.9 11.9 %multiply_reduce_fusion = (f32[1024]{0:T(1024)}, f32[1024]{0:T(1024)S(1)}, f32[1024,1024]{1,0:T(8,128)}) fusion(f32[1024,1024]{1,0:T(8,128)} %get-tuple-element.489, f32[1024]{0:T(1024)S(1)} %get-tuple-element.487, f32[1024]{0:T(1024)S(1)} %copy-done.22, bf16[1024,2048]{1,0:T(8,128)(2,1)} %all-gather.5.cloned.1.call-done, bf16[1024,2048]{1,0:T(8,128)(2,1)} %param.37), kind=kOutput, calls=%fused_computation.69 | convolution fusion | flops 4301256704 | bytes 16793600 | tf_op jit(solution)/shard_map/dot_general | solution.py:89
  200.8 5.8 psum.99
  206.6 9.2 fusion.28
  221.1 5.6 reshape.730
  226.8 5.6 reshape.729
  234.0 8.3 while.48
  242.3 28.5 %fusion.11 = (f32[4,256,16]{1,2,0:T(8,128)S(1)}, f32[4,256,16]{1,2,0:T(8,128)}, f32[4,256,256]{2,1,0:T(8,128)}) fusion(f32[4,256,16]{1,2,0:T(8,128)S(1)} %copy-done.31, f32[4,256,256]{2,1,0:T(8,128)} %fusion.132, pred[256,256]{1,0:T(8,128)(4,1)S(1)} %copy-done.29, f32[4,256,16,64]{1,3,2,0:T(8,128)} %copy.274, f32[4,256,16]{1,2,0:T(8,128)S(1)} %bitcast.319, ...), kind=kOutput, calls=%fused_computation.27 | convolution fusion | flops 3269165056 | bytes 10813504 | tf_op jit(solution)/shard_map/transpose(jvp(vmap(cijh,cjhp->cihp)))/dot_general | solution.py:36
  276.8 6.2 multiply_reduce_fusion.5
  284.6 9.2 while.49
  300.9 21.2 %fusion.29 = (f32[4,256,16]{1,2,0:T(8,128)S(1)}, f32[4,256,16]{1,2,0:T(8,128)}, f32[1,4,256,16,64]{2,4,3,1,0:T(8,128)}, f32[1,4,256,16,64]{2,4,3,1,0:T(8,128)}) fusion(f32[4,16,64,256]{3,2,1,0:T(8,128)S(1)} %fusion.56, f32[1,4,256,16,64]{2,4,3,1,0:T(8,128)S(1)} %copy-done.8, f32[4,256,16]{1,2,0:T(8,128)S(1)} %bitcast.320, f32[16]{0:T(128)S(1)} %copy-done.57, ...), kind=kOutput, calls=%fused_computation.61 | convolution fusion | flops 3253698560 | bytes 35061888 | tf_op jit(solution)/shard_map/transpose(jvp(vmap(cijh,cjhp->cihp)))/dot_general | solution.py:36
  324.6 9.9 reduce-window.16
  336.1 8.1 copy.326
  344.2 7.6 reshape.752
  351.8 12.2 %multiply_reduce_fusion.3 = (f32[1024]{0:T(1024)S(1)}, f32[1024]{0:T(1024)S(1)}, f32[1024]{0:T(1024)S(1)}, f32[1024]{0:T(1024)S(1)}, f32[1024]{0:T(1024)S(1)}, /*index=5*/f32[1,1024,1024]{2,1,0:T(8,128)}) fusion(f32[1,1024,1024]{2,1,0:T(8,128)} %bitcast.295, f32[1024,1024]{1,0:T(8,128)} %copy-done.2, f32[1,1024,1024]{2,1,0:T(8,128)} %get-tuple-element.493, ...), kind=kLoop, calls=%fused_computation.72 | loop fusion | flops 19917824 | bytes 20996096 | tf_op jit(solution)/shard_map/transpose(jvp(vmap()))/reduce_sum | solution.py:19
  364.0 8.1 copy.325
  372.1 7.6 reshape.751
  379.7 7.4 fusion.24
  387.2 6.7 fusion.133
  393.9 5.5 broadcast_multiply_fusion
  399.4 7.0 fusion.44
  406.4 7.2 fusion.134
  418.8 13.0 %fusion.119 = f32[1024,2048]{1,0:T(8,128)} fusion(bf16[1024,2048]{1,0:T(8,128)(2,1)} %param.37, f32[1024,1024]{1,0:T(8,128)} %get-tuple-element.489, f32[1024]{0:T(1024)S(1)} %copy-done.22, f32[1024]{0:T(1024)S(1)} %get-tuple-element.487), kind=kOutput, calls=%fused_computation.208 | convolution fusion | flops 4298113024 | bytes 16785408 | tf_op jit(solution)/shard_map/dot_general | solution.py:161
  434.4 7.1 fusion.88
  441.8 10.7 fusion.80
  458.1 42.2 %all-reduce.25 = (bf16[1024,256]{1,0:T(8,128)(2,1)S(1)}, f32[4,256]{1,0:T(4,128)S(1)}, f32[256]{0:T(256)S(1)}) all-reduce(f32[1024,256]{1,0:T(8,128)S(1)} %fusion.95, f32[4,256]{1,0:T(4,128)S(1)} %pad_add_fusion.7, f32[256]{0:T(256)S(1)} %get-tuple-element.429), channel_id=1, replica_groups=mesh['dp'=8,'head'=4] {'head'}, use_global_device_ids=true, to_apply=%region_25.26 | all-reduce | flops 263424 | bytes 1583104 | tf_op jit(solution)/shard_map/psum | solution.py:188
  505.6 11.6 fusion.118
  517.3 11.4 fusion.135
  529.0 10.6 fusion.136
  540.6 37.5 %all-reduce.22 = (f32[4,1024]{1,0:T(4,128)}, f32[1024]{0:T(1024)}, f32[4,256]{1,0:T(4,128)}, f32[256]{0:T(256)}, f32[16]{0:T(128)}, /*index=5*/f32[16]{0:T(128)}, f32[16]{0:T(128)}, f32[1024]{0:T(1024)}) all-reduce(f32[4,1024]{1,0:T(4,128)S(1)} %pad_add_fusion.6, ...), channel_id=1, replica_groups=mesh['dp'=8,'head'=4] {'dp'}, use_global_device_ids=true, to_apply=%region_37.38 | all-reduce | flops 7472 | bytes 59776 | tf_op jit(solution)/shard_map/psum | solution.py:228
  581.8 36.9 %psum.101 = f32[2048]{0:T(1024)} all-reduce(f32[2048]{0:T(1024)S(1)} %get-tuple-element.424), channel_id=1, replica_groups=mesh['dp'=8,'head'=4] {'dp','head'}, use_global_device_ids=true, to_apply=%region_28.29 | all-reduce | flops 2048 | bytes 16384 | tf_op jit(solution)/shard_map/psum | solution.py:218
  623.5 24.9 %reduce-scatter.18.cloned.1.call-done = f32[256,16]{0,1:T(8,128)} async-done(((f32[2048,16]{0,1:T(8,128)}), f32[256,16]{0,1:T(8,128)}) %reduce-scatter.18.cloned.1.call-update) | async-done | bytes 16400 | tf_op jit(solution)/shard_map/reduce_scatter | solution.py:245
  648.3 70.9 %reduce-scatter.16.cloned.1.call-done = f32[256,256]{1,0:T(8,128)} async-done(((f32[2048,256]{1,0:T(8,128)}), f32[256,256]{1,0:T(8,128)}) %reduce-scatter.16.cloned.1.call-update) | async-done | bytes 262160 | tf_op jit(solution)/shard_map/reduce_scatter | solution.py:244
  719.3 152.6 %reduce-scatter.20.cloned.1.call-done = f32[1024,256]{1,0:T(8,128)} async-done(((f32[1024,2048]{1,0:T(8,128)}), f32[1024,256]{1,0:T(8,128)}) %reduce-scatter.20.cloned.1.call-update) | async-done | bytes 1048592 | tf_op jit(solution)/shard_map/reduce_scatter | solution.py:246
  871.9 152.7 %reduce-scatter.12.cloned.1.call-done = f32[256,1024]{1,0:T(8,128)} async-done(((f32[2048,1024]{1,0:T(8,128)}), f32[256,1024]{1,0:T(8,128)}) %reduce-scatter.12.cloned.1.call-update) | async-done | bytes 1048592 | tf_op jit(solution)/shard_map/reduce_scatter | solution.py:242
  1024.5 152.3 %reduce-scatter.14.cloned.1.call-done = f32[256,1024]{1,0:T(8,128)} async-done(((f32[2048,1024]{1,0:T(8,128)}), f32[256,1024]{1,0:T(8,128)}) %reduce-scatter.14.cloned.1.call-update) | async-done | bytes 1048592 | tf_op jit(solution)/shard_map/reduce_scatter | solution.py:243
  (298 shorter events, 114.9 us)
Async XLA Ops:
  7.2 50.8 %copy-start = (bf16[2048,256]{1,0:T(8,128)(2,1)S(1)}, bf16[2048,256]{1,0:T(8,128)(2,1)}, u32[]{:S(2)}) copy-start(bf16[2048,256]{1,0:T(8,128)(2,1)} %param.27) | copy-start | bytes 3145732
  7.2 8.2 copy-start.46
  7.2 42.1 %copy-start.24 = (bf16[2048,16]{0,1:T(8,128)(2,1)S(1)}, bf16[2048,16]{0,1:T(8,128)(2,1)}, u32[]{:S(2)}) copy-start(bf16[2048,16]{0,1:T(8,128)(2,1)} %param.28) | copy-start | bytes 196612
  7.2 42.1 %copy-start.62 = (f32[16]{0:T(128)S(1)}, f32[16]{0:T(128)}, u32[]{:S(2)}) copy-start(f32[16]{0:T(128)} %param.33) | copy-start | bytes 196
  7.3 42.1 %all-gather.3.cloned.1.call-start = ((), (), s32[]{:S(2)}) async-start(), calls=%async_computation.7 | async-start | bytes 5242880 | tf_op jit(solution)/shard_map/all_gather | solution.py:122
  12.0 176.9 %all-gather.5.cloned.1.call-start = ((), (), s32[]{:S(2)}) async-start(), calls=%async_computation.9 | async-start | bytes 5242880 | tf_op jit(solution)/shard_map/all_gather | solution.py:167
  12.7 565.3 %reduce-scatter.10.cloned.1.call-start = ((), (), s32[]{:S(2)}) async-start(), calls=%async_computation.10 | async-start | bytes 10485760 | tf_op jit(solution)/shard_map/reduce_scatter | solution.py:195
  14.1 39.2 %copy-start.63 = (f32[16]{0:T(128)}, f32[16]{0:T(128)S(1)}, u32[]{:S(2)}) copy-start(f32[16]{0:T(128)S(1)} %exponential_negate_fusion) | copy-start | bytes 196
  14.6 47.5 %copy-start.48 = (f32[1,256]{1,0:T(1,128)}, f32[1,256]{1,0:T(1,128)S(1)}, u32[]{:S(2)}) copy-start(f32[1,256]{1,0:T(1,128)S(1)} %get-tuple-element.518) | copy-start | bytes 3076
  14.6 47.5 %copy-start.50 = (f32[1,256]{1,0:T(1,128)}, f32[1,256]{1,0:T(1,128)S(1)}, u32[]{:S(2)}) copy-start(f32[1,256]{1,0:T(1,128)S(1)} %get-tuple-element.519) | copy-start | bytes 3076
  14.6 47.5 %copy-start.52 = (f32[1,256]{1,0:T(1,128)}, f32[1,256]{1,0:T(1,128)S(1)}, u32[]{:S(2)}) copy-start(f32[1,256]{1,0:T(1,128)S(1)} %get-tuple-element.520) | copy-start | bytes 3076
  14.6 47.5 %copy-start.54 = (f32[1,256]{1,0:T(1,128)}, f32[1,256]{1,0:T(1,128)S(1)}, u32[]{:S(2)}) copy-start(f32[1,256]{1,0:T(1,128)S(1)} %get-tuple-element.521) | copy-start | bytes 3076
  15.4 55.8 %copy-start.32 = (f32[1,1024]{1,0:T(1,128)}, f32[1,1024]{1,0:T(1,128)S(1)}, u32[]{:S(2)}) copy-start(f32[1,1024]{1,0:T(1,128)S(1)} %get-tuple-element.514) | copy-start | bytes 12292
  15.4 55.8 %copy-start.34 = (f32[1,1024]{1,0:T(1,128)}, f32[1,1024]{1,0:T(1,128)S(1)}, u32[]{:S(2)}) copy-start(f32[1,1024]{1,0:T(1,128)S(1)} %get-tuple-element.515) | copy-start | bytes 12292
  15.4 55.8 %copy-start.36 = (f32[1,1024]{1,0:T(1,128)}, f32[1,1024]{1,0:T(1,128)S(1)}, u32[]{:S(2)}) copy-start(f32[1,1024]{1,0:T(1,128)S(1)} %get-tuple-element.516) | copy-start | bytes 12292
  15.4 55.8 %copy-start.38 = (f32[1,1024]{1,0:T(1,128)}, f32[1,1024]{1,0:T(1,128)S(1)}, u32[]{:S(2)}) copy-start(f32[1,1024]{1,0:T(1,128)S(1)} %get-tuple-element.517) | copy-start | bytes 12292
  57.4 18.5 %copy-start.41 = (f32[4,16]{1,0:T(4,128)}, f32[4,16]{1,0:T(4,128)S(1)}, u32[]{:S(2)}) copy-start(f32[4,16]{1,0:T(4,128)S(1)} %get-tuple-element.431) | copy-start | bytes 772
  98.3 7.9 copy-start.57
  106.2 7.9 copy-start.4
  106.2 7.9 copy-start.20
  106.2 7.9 copy-start.28
  106.3 7.8 copy-start.30
  114.1 22.0 %copy-start.65 = (f32[4,16]{1,0:T(4,128)S(1)}, f32[4,16]{1,0:T(4,128)}, u32[]{:S(2)}) copy-start(f32[4,16]{1,0:T(4,128)} %get-tuple-element.432) | copy-start | bytes 772
  136.1 8.5 copy-start.67
  170.3 18.5 %copy-start.22 = (f32[1024]{0:T(1024)S(1)}, f32[1024]{0:T(1024)}, u32[]{:S(2)}) copy-start(f32[1024]{0:T(1024)} %param.36) | copy-start | bytes 12292
  188.8 17.7 %copy-start.40 = (f32[1024]{0:T(1024)S(1)}, f32[1024]{0:T(1024)}, u32[]{:S(2)}) copy-start(f32[1024]{0:T(1024)} %mul.823) | copy-start | bytes 12292
  234.0 8.3 copy-start.29
  234.0 8.3 copy-start.31
  242.3 29.1 %copy-start.1 = (f32[4,256,16,64]{1,0,3,2:T(4,128)S(1)}, f32[4,256,16,64]{1,0,3,2:T(4,128)}, u32[]{:S(2)}) copy-start(f32[4,256,16,64]{1,0,3,2:T(4,128)} %reshape.730) | copy-start | bytes 12582916
  284.6 11.0 copy-start.13
  300.9 21.8 %copy-start.42 = (f32[4,16]{1,0:T(4,128)S(1)}, f32[4,16]{1,0:T(4,128)}, u32[]{:S(2)}) copy-start(f32[4,16]{1,0:T(4,128)} %copy-done.41) | copy-start | bytes 772
  300.9 34.1 %copy-start.64 = (f32[16]{0:T(128)S(1)}, f32[16]{0:T(128)}, u32[]{:S(2)}) copy-start(f32[16]{0:T(128)} %copy-done.63) | copy-start | bytes 196
  399.4 14.4 %slice-start = ((s8[8388608]{0:T(1024)(128)(4,1)}), s8[4194304]{0:T(1024)(128)(4,1)S(1)}, s32[]{:S(2)}) async-start(s8[8388608]{0:T(1024)(128)(4,1)} %bitcast.307), calls=%async_computation.16 | async-start | bytes 8388608
  406.4 7.4 slice-start.1
  418.5 200.3 %reduce-scatter.8.cloned.1.call-start = ((), (), s32[]{:S(2)}) async-start(), calls=%async_computation.8 | async-start | bytes 10485760 | tf_op jit(solution)/shard_map/reduce_scatter | solution.py:160
  431.8 216.5 %reduce-scatter.18.cloned.1.call-start = ((), (), s32[]{:S(2)}) async-start(), calls=%async_computation.14 | async-start | bytes 147456 | tf_op jit(solution)/shard_map/reduce_scatter | solution.py:245
  441.7 10.7 copy-start.17
  441.7 11.8 copy-start.10
  441.7 11.8 copy-start.15
  458.0 261.3 %reduce-scatter.16.cloned.1.call-start = ((), (), s32[]{:S(2)}) async-start(), calls=%async_computation.13 | async-start | bytes 2359296 | tf_op jit(solution)/shard_map/reduce_scatter | solution.py:244
  505.4 366.5 %reduce-scatter.20.cloned.1.call-start = ((), (), s32[]{:S(2)}) async-start(), calls=%async_computation.15 | async-start | bytes 9437184 | tf_op jit(solution)/shard_map/reduce_scatter | solution.py:246
  517.3 507.3 %reduce-scatter.12.cloned.1.call-start = ((), (), s32[]{:S(2)}) async-start(), calls=%async_computation.11 | async-start | bytes 9437184 | tf_op jit(solution)/shard_map/reduce_scatter | solution.py:242
  528.7 648.1 %reduce-scatter.14.cloned.1.call-start = ((), (), s32[]{:S(2)}) async-start(), calls=%async_computation.12 | async-start | bytes 9437184 | tf_op jit(solution)/shard_map/reduce_scatter | solution.py:243
  539.6 38.4 %copy-start.7 = (bf16[256,2048]{1,0:T(8,128)(2,1)S(1)}, bf16[256,2048]{1,0:T(8,128)(2,1)}, u32[]{:S(2)}) copy-start(bf16[256,2048]{1,0:T(8,128)(2,1)} %param.23) | copy-start | bytes 3145732
  539.6 38.4 %copy-start.27 = (f32[2048]{0:T(1024)S(1)}, f32[2048]{0:T(1024)}, u32[]{:S(2)}) copy-start(f32[2048]{0:T(1024)} %param.24) | copy-start | bytes 24580
  539.7 38.4 %copy-start.45 = (f32[256]{0:T(256)S(1)}, f32[256]{0:T(256)}, u32[]{:S(2)}) copy-start(f32[256]{0:T(256)} %copy-done.44) | copy-start | bytes 3076
  539.7 79.1 %copy-start.14 = (bf16[256,2048]{1,0:T(8,128)(2,1)S(1)}, bf16[256,2048]{1,0:T(8,128)(2,1)}, u32[]{:S(2)}) copy-start(bf16[256,2048]{1,0:T(8,128)(2,1)} %param.38) | copy-start | bytes 3145732
  539.7 79.1 %copy-start.58 = (f32[256]{0:T(256)S(1)}, f32[256]{0:T(256)}, u32[]{:S(2)}) copy-start(f32[256]{0:T(256)} %get-tuple-element.522) | copy-start | bytes 3076
  (36 other events, 161.3 us)
Sparse Core Ops, SparseCore 0:
  12.1 37.1 all-gather.2
  50.9 34.4 all-gather.4
  418.6 90.2 reduce-scatter.9
  511.5 71.6 reduce-scatter.7
  587.0 61.2 reduce-scatter.17
  652.3 66.9 reduce-scatter.15
  723.5 148.3 reduce-scatter.19
  876.5 147.9 reduce-scatter.11
  1028.8 148.0 reduce-scatter.13
where the time goes:
time: 1200 us; the launch traced here: 1180 us
  waiting for transfers between devices  588 us (49%)
  matrix products  239 us (20%)
  blocking collectives  128 us (11%)
  local copies, waits for them, and re-layouts  109 us (9%)
  other arithmetic  101 us (8%)
  between operations  15.9 us (1%)
    reduce_scatter x1, waiting for transfers between devices, per_device(): lax.psum_scatter(gate_part, 'dp', scatter_dimension=0, tiled=True)  153 us
    reduce_scatter x1, waiting for transfers between devices, per_device(): lax.psum_scatter(out_proj_part, 'dp', scatter_dimension=1, tiled=True)  153 us
    reduce_scatter x1, waiting for transfers between devices, per_device(): lax.psum_scatter(value_part, 'dp', scatter_dimension=0, tiled=True)  152 us
    reduce_scatter x1, waiting for transfers between devices, per_device(): lax.psum_scatter(state_part, 'dp', scatter_dimension=0, tiled=True)  70.9 us
    dot_general x3, matrix products, state_space(): within = jnp.einsum('cijh,cjhp->cihp', mixing, scaled, precision=HIGH)  70 us
    psum x1, blocking collectives, per_device(): lax.psum((d_state_pre, g_conv_state, g_conv_state_bias), 'head')  42.2 us
    dot_general x5, matrix products, contract_rows(): lax.dot_general(left, right, (((0,), (0,)), ((), ())), preferred_element_...  40 us
    psum x1, blocking collectives, per_device(): lax.psum((g_conv_value, g_conv_value_bias, g_step_bias, g_decay_log, g_sk...  37.5 us
  transfers between devices with their start and end apart: 9, of which 6 were waited for; matrix products, arithmetic and copies ran while one was open for 18% of the time, Pallas kernels for 0%

commit v1 on v0

v1 whole, which is shorter than its diff:
```python
import functools
import jax
import jax.numpy as jnp
from jax import lax
from jax.experimental import pallas as pl
from jax.experimental.pallas import tpu as pltpu
from jax.sharding import PartitionSpec as P

F32 = jnp.float32
BF = jnp.bfloat16
LANES = 128
EPS = 1e-05


def mm(a, b):
    return jnp.dot(a, b, preferred_element_type=F32)


def mm_t(a, b):
    return lax.dot_general(a, b, (((1,), (1,)), ((), ())), preferred_element_type=F32)


def t_mm(a, b):
    return lax.dot_general(a, b, (((0,), (0,)), ((), ())), preferred_element_type=F32)


def sigmoid(v):
    return 0.5 * jnp.tanh(0.5 * v) + 0.5


def softplus(v):
    return jnp.maximum(v, 0.0) + jnp.log1p(jnp.exp(-jnp.abs(v)))


def split3(v):
    hi = v.astype(BF)
    rest = v - hi.astype(F32)
    mid = rest.astype(BF)
    low = (rest - mid.astype(F32)).astype(BF)
    return hi, mid, low


def split2(v):
    hi = v.astype(BF)
    return hi, (v - hi.astype(F32)).astype(BF)


def exact_left(ones, v):
    hi, mid, low = split3(v)
    return mm(ones, hi) + mm(ones, mid) + mm(ones, low)


def conv(buf, first, taps, length):
    out = taps[0][None] * buf[pl.ds(first, length), :]
    for k in range(1, len(taps)):
        out = out + taps[k][None] * buf[pl.ds(first + k, length), :]
    return out


def scan_parts(step_pre, bias, rate, span):
    raw = step_pre + bias
    size = softplus(raw)
    row = lax.broadcasted_iota(jnp.int32, (span, span), 0)
    col = lax.broadcasted_iota(jnp.int32, (span, span), 1)
    tri = (row >= col).astype(BF)
    cum = exact_left(tri, size * rate)
    return raw, size, cum, row, col


def spread_heads(values, expand):
    hi, low = split2(values)
    return mm(hi, expand) + mm(low, expand)


def fwd_kernel(
    span, heads, taps_n, vp_ref, ss_ref, cv_ref, cs_ref, hv_ref, ex_ref,
    ssd_ref, ent_ref, state, vbuf, sbuf,
):
    chans = vp_ref.shape[1]
    maps = cs_ref.shape[1]
    nst = maps // 2
    halo = taps_n - 1

    @pl.when(pl.program_id(0) == 0)
    def _():
        state[...] = jnp.zeros_like(state)
        vbuf[0:8, :] = jnp.zeros((8, chans), F32)
        sbuf[0:8, :] = jnp.zeros((8, maps), F32)

    vbuf[8 : 8 + span, :] = vp_ref[...].astype(F32)
    sbuf[8 : 8 + span, :] = ss_ref[:, :maps]
    taps = [cv_ref[k] for k in range(taps_n)]
    pre = conv(vbuf, 8 - halo, taps, span) + cv_ref[4][None]
    staps = [cs_ref[k] for k in range(taps_n)]
    spre = conv(sbuf, 8 - halo, staps, span) + cs_ref[4][None]
    vbuf[0:8, :] = vbuf[span : span + 8, :]
    sbuf[0:8, :] = sbuf[span : span + 8, :]
    sact = spre * sigmoid(spre)
    key = sact[:, :nst].astype(BF)
    query = sact[:, nst:].astype(BF)
    x = pre * sigmoid(pre) * cv_ref[6][None]
    _, size, cum, row, col = scan_parts(ss_ref[:, maps:], hv_ref[0][None], hv_ref[1][None], span)
    expand = ex_ref[...]
    last = cum[span - 1 : span, :]
    size_e = spread_heads(size, expand)
    ecum_e = spread_heads(jnp.exp(cum), expand)
    tail_e = spread_heads(jnp.exp(last - cum), expand)
    etot_e = spread_heads(jnp.broadcast_to(jnp.exp(last), (8, LANES)), expand)[0:1]
    xs = x * size_e
    xs_low = xs.astype(BF)
    before = state[...]
    before_low = before.astype(BF)
    ent_ref[0] = before_low
    inter = mm(query, before_low) * ecum_e
    state[...] = before * etot_e + t_mm(key, (xs * tail_e).astype(BF))
    inner = mm_t(query, key)
    cum_t = jnp.transpose(cum)
    keepm = row >= col
    left = lax.broadcasted_iota(jnp.int32, (span, LANES), 1) < LANES // 2
    for pair in range(heads // 2):
        lanes = slice(pair * LANES, (pair + 1) * LANES)
        part = []
        for h in (2 * pair, 2 * pair + 1):
            diff = cum[:, h : h + 1] - cum_t[h : h + 1, :]
            mix = jnp.exp(jnp.where(keepm, diff, -1e30)) * inner
            part.append(mm(mix.astype(BF), xs_low[:, lanes]))
        within = jnp.where(left, part[0], part[1])
        ssd_ref[:, lanes] = (within + inter[:, lanes] + x[:, lanes] * cv_ref[5:6, lanes]).astype(ssd_ref.dtype)


def bwd_kernel(
    span, heads, taps_n, vp_ref, vh_ref, ss_ref, sh_ref, dy_ref, ent_ref, cv_ref, cs_ref, hv_ref, ex_ref,
    dv_ref, ds_ref, gcv_ref, gcs_ref, gh_ref, dstate, vbuf, sbuf, dvbuf, dsbuf,
):
    chans = vp_ref.shape[1]
    maps = cs_ref.shape[1]
    nst = maps // 2
    halo = taps_n - 1
    step = pl.program_id(0)
    first = step == 0
    start = step == pl.num_programs(0) - 1

    @pl.when(first)
    def _():
        dstate[...] = jnp.zeros_like(dstate)
        dvbuf[span : span + 8, :] = jnp.zeros((8, chans), F32)
        dsbuf[span : span + 8, :] = jnp.zeros((8, maps), F32)
        gcv_ref[...] = jnp.zeros_like(gcv_ref)
        gcs_ref[...] = jnp.zeros_like(gcs_ref)
        gh_ref[...] = jnp.zeros_like(gh_ref)

    vbuf[0:8, :] = jnp.where(start, 0.0, vh_ref[...].astype(F32))
    sbuf[0:8, :] = jnp.where(start, 0.0, sh_ref[:, :maps])
    vbuf[8 : 8 + span, :] = vp_ref[...].astype(F32)
    sbuf[8 : 8 + span, :] = ss_ref[:, :maps]
    taps = [cv_ref[k] for k in range(taps_n)]
    pre = conv(vbuf, 8 - halo, taps, span) + cv_ref[4][None]
    staps = [cs_ref[k] for k in range(taps_n)]
    spre = conv(sbuf, 8 - halo, staps, span) + cs_ref[4][None]
    ssig = sigmoid(spre)
    sact = spre * ssig
    key = sact[:, :nst].astype(BF)
    query = sact[:, nst:].astype(BF)
    sig = sigmoid(pre)
    keep = cv_ref[6][None]
    x = pre * sig * keep
    rate = hv_ref[1][None]
    raw, size, cum, row, col = scan_parts(ss_ref[:, maps:], hv_ref[0][None], rate, span)
    expand = ex_ref[...]
    last = cum[span - 1 : span, :]
    size_e = spread_heads(size, expand)
    ecum_e = spread_heads(jnp.exp(cum), expand)
    tail_e = spread_heads(jnp.exp(last - cum), expand)
    etot_e = spread_heads(jnp.broadcast_to(jnp.exp(last), (8, LANES)), expand)[0:1]
    xs = x * size_e
    xs_low = xs.astype(BF)
    xt = xs * tail_e
    xt_low = xt.astype(BF)
    dy_low = dy_ref[...].astype(BF)
    dy = dy_low.astype(F32)
    before_low = ent_ref[0]
    dz = dy * ecum_e
    dz_low = dz.astype(BF)
    d_after = dstate[...]
    d_after_low = d_after.astype(BF)
    inter = mm(query, before_low)
    w = mm(key, d_after_low)
    d_query = mm_t(dz_low, before_low)
    d_key = mm_t(xt_low, d_after_low)
    through = jnp.sum(d_after * before_low.astype(F32), axis=0, keepdims=True) * etot_e
    dstate[...] = d_after * etot_e + t_mm(query, dz_low)
    inner_t = mm_t(key, query)
    cum_t = jnp.transpose(cum)
    keepm = row <= col
    lane = lax.broadcasted_iota(jnp.int32, (span, LANES), 1)
    left = lane < LANES // 2
    d_inner_t = jnp.zeros((span, span), F32)
    cols = jnp.zeros((span, LANES), F32)
    rows = []
    dxs_parts = []
    zero = jnp.zeros((span, LANES), BF)
    for pair in range(heads // 2):
        lanes = slice(pair * LANES, (pair + 1) * LANES)
        part = []
        xp = xs_low[:, lanes]
        dyp = dy_low[:, lanes]
        for h, mine in ((2 * pair, left), (2 * pair + 1, jnp.logical_not(left))):
            diff = cum_t[h : h + 1, :] - cum[:, h : h + 1]
            decay = jnp.exp(jnp.where(keepm, diff, -1e30))
            mix = decay * inner_t
            part.append(mm(mix.astype(BF), dyp))
            d_mix = mm_t(jnp.where(mine, xp, zero), dyp) * decay
            d_inner_t = d_inner_t + d_mix
            seg = d_mix * inner_t
            rows.append(jnp.sum(seg, axis=0, keepdims=True))
            cols = cols + jnp.where(lane == h, jnp.sum(seg, axis=1, keepdims=True), 0.0)
        dxs_parts.append(jnp.where(left, part[0], part[1]))
    rows.append(jnp.zeros((LANES - heads, span), F32))
    row_sums = jnp.transpose(jnp.concatenate(rows, axis=0))
    dxs = jnp.concatenate(dxs_parts, axis=1) + w * tail_e
    d_inner_low = d_inner_t.astype(BF)
    d_key = d_key + mm(d_inner_low, query)
    d_query = d_query + t_mm(d_inner_low, key)

    gather = functools.partial(mm_t, b=expand)
    r_inter = gather((dz * inter).astype(BF))
    c_tail = gather((xt * w).astype(BF))
    d_size = gather((dxs * x).astype(BF))
    d_skip = gather((dy * x).astype(BF))
    d_tot = gather(jnp.broadcast_to(through, (8, chans)).astype(BF))[0:1]
    later = (row <= col).astype(BF)
    earlier = (row > col).astype(BF)
    d_la = exact_left(later, row_sums - cols + r_inter) + exact_left(earlier, c_tail) + d_tot
    d_step = (d_size + rate * d_la) * sigmoid(raw)
    gh_ref[0:1, :] = gh_ref[0:1, :] + jnp.sum(d_step, axis=0, keepdims=True)
    gh_ref[1:2, :] = gh_ref[1:2, :] + jnp.sum(d_la * size, axis=0, keepdims=True) * rate
    gh_ref[2:3, :] = gh_ref[2:3, :] + jnp.sum(d_skip, axis=0, keepdims=True)

    d_pre = (dxs * size_e + dy * cv_ref[5][None]) * keep * (sig * (1.0 + pre * (1.0 - sig)))
    dvbuf[0:span, :] = d_pre
    dv = taps[taps_n - 1][None] * d_pre
    for k in range(taps_n - 1):
        dv = dv + taps[k][None] * dvbuf[pl.ds(halo - k, span), :]
    dv_ref[...] = dv.astype(dv_ref.dtype)
    for k in range(taps_n):
        gcv_ref[k : k + 1, :] = gcv_ref[k : k + 1, :] + jnp.sum(
            d_pre * vbuf[pl.ds(8 - halo + k, span), :], axis=0, keepdims=True
        )
    gcv_ref[4:5, :] = gcv_ref[4:5, :] + jnp.sum(d_pre, axis=0, keepdims=True)
    dvbuf[span : span + 8, :] = dvbuf[0:8, :]

    d_spre = jnp.concatenate([d_key, d_query], axis=1) * (ssig * (1.0 + spre * (1.0 - ssig)))
    dsbuf[0:span, :] = d_spre
    dsv = staps[taps_n - 1][None] * d_spre
    for k in range(taps_n - 1):
        dsv = dsv + staps[k][None] * dsbuf[pl.ds(halo - k, span), :]
    ds_ref[:, :maps] = dsv.astype(ds_ref.dtype)
    ds_ref[:, maps:] = d_step.astype(ds_ref.dtype)
    for k in range(taps_n):
        gcs_ref[k : k + 1, :] = gcs_ref[k : k + 1, :] + jnp.sum(
            d_spre * sbuf[pl.ds(8 - halo + k, span), :], axis=0, keepdims=True
        )
    gcs_ref[4:5, :] = gcs_ref[4:5, :] + jnp.sum(d_spre, axis=0, keepdims=True)
    dsbuf[span : span + 8, :] = dsbuf[0:8, :]


def full(shape):
    return pl.BlockSpec(shape, lambda i: (0,) * len(shape))


def scan_fwd(vp, ss, cv, cs, hv, ex, heads, taps_n, span):
    rows, chans = vp.shape
    wide = ss.shape[1]
    maps = cs.shape[1]
    nb = rows // span
    return pl.pallas_call(
        functools.partial(fwd_kernel, span, heads, taps_n),
        grid=(nb,),
        in_specs=[
            pl.BlockSpec((span, chans), lambda i: (i, 0)),
            pl.BlockSpec((span, wide), lambda i: (i, 0)),
            full(cv.shape), full(cs.shape), full(hv.shape), full(ex.shape),
        ],
        out_specs=[
            pl.BlockSpec((span, chans), lambda i: (i, 0)),
            pl.BlockSpec((1, maps // 2, chans), lambda i: (i, 0, 0)),
        ],
        out_shape=[
            jax.ShapeDtypeStruct((rows, chans), F32),
            jax.ShapeDtypeStruct((nb, maps // 2, chans), BF),
        ],
        scratch_shapes=[
            pltpu.VMEM((maps // 2, chans), F32),
            pltpu.VMEM((span + 8, chans), F32),
            pltpu.VMEM((span + 8, maps), F32),
        ],
        compiler_params=pltpu.CompilerParams(
            dimension_semantics=("arbitrary",), vmem_limit_bytes=40 << 20),
        name="scan_fwd",
    )(vp, ss, cv, cs, hv, ex)


def scan_bwd(vp, ss, dy, ent, cv, cs, hv, ex, heads, taps_n, span):
    rows, chans = vp.shape
    wide = ss.shape[1]
    maps = cs.shape[1]
    nb = rows // span
    eights = span // 8
    back = lambda i: (nb - 1 - i, 0)
    halo = lambda i: (jnp.maximum((nb - 1 - i) * eights - 1, 0), 0)
    return pl.pallas_call(
        functools.partial(bwd_kernel, span, heads, taps_n),
        grid=(nb,),
        in_specs=[
            pl.BlockSpec((span, chans), back),
            pl.BlockSpec((8, chans), halo),
            pl.BlockSpec((span, wide), back),
            pl.BlockSpec((8, wide), halo),
            pl.BlockSpec((span, chans), back),
            pl.BlockSpec((1, maps // 2, chans), lambda i: (nb - 1 - i, 0, 0)),
            full(cv.shape), full(cs.shape), full(hv.shape), full(ex.shape),
        ],
        out_specs=[
            pl.BlockSpec((span, chans), back),
            pl.BlockSpec((span, wide), back),
            full((8, chans)), full((8, maps)), full((8, LANES)),
        ],
        out_shape=[
            jax.ShapeDtypeStruct((rows, chans), BF),
            jax.ShapeDtypeStruct((rows, wide), BF),
            jax.ShapeDtypeStruct((8, chans), F32),
            jax.ShapeDtypeStruct((8, maps), F32),
            jax.ShapeDtypeStruct((8, LANES), F32),
        ],
        scratch_shapes=[
            pltpu.VMEM((maps // 2, chans), F32),
            pltpu.VMEM((span + 8, chans), F32),
            pltpu.VMEM((span + 8, maps), F32),
            pltpu.VMEM((span + 8, chans), F32),
            pltpu.VMEM((span + 8, maps), F32),
        ],
        compiler_params=pltpu.CompilerParams(
            dimension_semantics=("arbitrary",), vmem_limit_bytes=48 << 20),
        name="scan_bwd",
    )(vp, vp, ss, ss, dy, ent, cv, cs, hv, ex)


def tables(conv_value, conv_value_bias, conv_state, conv_state_bias, step_bias, decay_log, skip_gain, keep, out_gain):
    heads = step_bias.shape[0]
    chans = conv_value.shape[1]
    head_dim = chans // heads
    row = lambda v: v[None, :]
    wide = lambda v: jnp.repeat(v, head_dim)[None, :]
    cv = jnp.concatenate([conv_value, row(conv_value_bias), wide(skip_gain), wide(keep), row(out_gain)], axis=0)
    cs = jnp.concatenate([conv_state, row(conv_state_bias), jnp.zeros((3, conv_state.shape[1]), F32)], axis=0)
    lanes = lambda v: jnp.pad(v, (0, LANES - heads))[None, :]
    hv = jnp.concatenate([lanes(step_bias), lanes(-jnp.exp(decay_log)), jnp.zeros((6, LANES), F32)], axis=0)
    head_of = lax.broadcasted_iota(jnp.int32, (LANES, chans), 1) // head_dim
    ex = (head_of == lax.broadcasted_iota(jnp.int32, (LANES, chans), 0)).astype(BF)
    return cv, cs, hv, ex


def sums_kernel(ssd_ref, gate_ref, dno_ref, cv_ref, out_ref):
    gate = gate_ref[...].astype(F32)
    gated = ssd_ref[...].astype(F32) * gate * sigmoid(gate)
    squares = jnp.sum(gated * gated, axis=1, keepdims=True)
    stat = jnp.sum(dno_ref[...].astype(F32) * cv_ref[7][None] * gated, axis=1, keepdims=True)
    lane = lax.broadcasted_iota(jnp.int32, (gated.shape[0], LANES), 1)
    both = jnp.where(lane == 0, squares, jnp.where(lane == 1, stat, 0.0))
    out_ref[...] = jnp.transpose(both)[0:8]


def row_sums_of(ssd, gate, dno, cv):
    rows, chans = ssd.shape
    span = 256
    tile = pl.BlockSpec((span, chans), lambda i: (i, 0))
    return pl.pallas_call(
        sums_kernel,
        grid=(rows // span,),
        in_specs=[tile, tile, tile, full(cv.shape)],
        out_specs=pl.BlockSpec((8, span), lambda i: (0, i)),
        out_shape=jax.ShapeDtypeStruct((8, rows), F32),
        compiler_params=pltpu.CompilerParams(
            dimension_semantics=("arbitrary",), vmem_limit_bytes=40 << 20),
        name="row_sums",
    )(ssd, gate, dno, cv)


def norm_kernel(ssd_ref, gate_ref, dno_ref, cv_ref, sums_ref, count_ref, no_ref, dy_ref, dg_ref, og_ref):
    @pl.when(pl.program_id(0) == 0)
    def _():
        og_ref[...] = jnp.zeros_like(og_ref)

    span = ssd_ref.shape[0]
    per = jnp.transpose(jnp.concatenate([sums_ref[...], jnp.zeros((LANES - 8, span), F32)], axis=0))
    count = count_ref[0, 0]
    scale = lax.rsqrt(per[:, 0:1] / count + EPS)
    coef = scale * scale * scale * (per[:, 1:2] / count)
    gate = gate_ref[...].astype(F32)
    ssd = ssd_ref[...].astype(F32)
    sig = sigmoid(gate)
    act = gate * sig
    gated = ssd * act
    gain = cv_ref[7][None]
    dno = dno_ref[...].astype(F32)
    unit = gated * scale
    no_ref[...] = (unit * gain).astype(no_ref.dtype)
    d_gated = dno * gain * scale - gated * coef
    dy_ref[...] = (d_gated * act).astype(dy_ref.dtype)
    dg_ref[...] = (d_gated * ssd * (sig * (1.0 + gate * (1.0 - sig)))).astype(dg_ref.dtype)
    og_ref[0:1, :] = og_ref[0:1, :] + jnp.sum(dno * unit, axis=0, keepdims=True)


def norm_both(ssd, gate, dno, cv, sums, count):
    rows, chans = ssd.shape
    span = 256
    tile = pl.BlockSpec((span, chans), lambda i: (i, 0))
    low = jax.ShapeDtypeStruct((rows, chans), BF)
    return pl.pallas_call(
        norm_kernel,
        grid=(rows // span,),
        in_specs=[
            tile, tile, tile, full(cv.shape),
            pl.BlockSpec((8, span), lambda i: (0, i)),
            pl.BlockSpec(memory_space=pltpu.SMEM),
        ],
        out_specs=[tile, tile, tile, full((8, chans))],
        out_shape=[low, low, low, jax.ShapeDtypeStruct((8, chans), F32)],
        compiler_params=pltpu.CompilerParams(
            dimension_semantics=("arbitrary",), vmem_limit_bytes=40 << 20),
        name="norm_both",
    )(ssd, gate, dno, cv, sums, count)


def per_device(
    hidden_in, in_gain, gate_proj, value_proj, state_proj, step_proj, conv_value, conv_value_bias,
    conv_state, conv_state_bias, step_bias, decay_log, skip_gain, out_gain, out_proj, cotangent, width_level,
):
    heads = step_bias.shape[0]
    chans = conv_value.shape[1]
    head_dim = chans // heads
    maps = conv_state.shape[1]
    taps_n = conv_value.shape[0]
    groups = lax.axis_size("head")
    model = hidden_in.shape[1]
    assert width_level.shape[0] == 1 and 2 * head_dim == LANES and heads <= LANES
    span = 128

    resid = hidden_in.astype(F32)
    in_scale = lax.rsqrt(jnp.mean(resid * resid, axis=-1, keepdims=True) + EPS)
    normed = (resid * in_scale * in_gain).astype(BF)
    whole = lax.all_gather(normed, "head", axis=0, tiled=True)
    cot_all = lax.all_gather(cotangent, "head", axis=0, tiled=True)
    side_proj = jnp.concatenate(
        [state_proj, step_proj, jnp.zeros((model, LANES - heads), BF)], axis=1)

    active = jnp.right_shift(heads, 3 - width_level[0])
    keep = (jnp.arange(heads) < active).astype(F32)
    count = (active * groups * head_dim).astype(F32).reshape(1, 1)
    cv, cs, hv, ex = tables(
        conv_value, conv_value_bias, conv_state, conv_state_bias, step_bias, decay_log, skip_gain, keep, out_gain)

    value_pre = mm(whole, value_proj)
    side_pre = mm(whole, side_proj)
    gate_pre = mm(whole, gate_proj)
    ssd, entering = scan_fwd(value_pre, side_pre, cv, cs, hv, ex, heads, taps_n, span)
    d_normed_out = mm_t(cot_all, out_proj)
    sums = row_sums_of(ssd, gate_pre, d_normed_out, cv)
    sums = jnp.pad(lax.psum(sums[:2], "head"), ((0, 6), (0, 0)))
    normed_out, dy, d_gate, og = norm_both(ssd, gate_pre, d_normed_out, cv, sums, count)
    out_part = mm(normed_out, out_proj).astype(BF)
    own_out = lax.psum_scatter(out_part, "head", scatter_dimension=0, tiled=True)
    out_proj_grad = lax.psum_scatter(
        t_mm(normed_out, cot_all).astype(BF), "dp", scatter_dimension=1, tiled=True).astype(F32)
    gate_proj_grad = lax.psum_scatter(
        t_mm(whole, d_gate).astype(BF), "dp", scatter_dimension=0, tiled=True).astype(F32)
    d_value, d_side, gcv, gcs, gh = scan_bwd(
        value_pre, side_pre, dy, entering, cv, cs, hv, ex, heads, taps_n, span)
    value_proj_grad = lax.psum_scatter(
        t_mm(whole, d_value).astype(BF), "dp", scatter_dimension=0, tiled=True).astype(F32)
    d_normed = (mm_t(d_gate, gate_proj) + mm_t(d_value, value_proj) + mm_t(d_side, side_proj)).astype(BF)
    d_normed = lax.psum_scatter(d_normed, "head", scatter_dimension=0, tiled=True).astype(F32)
    side_grad = lax.psum_scatter(
        t_mm(whole, d_side).astype(BF), "dp", scatter_dimension=0, tiled=True).astype(F32)
    step_proj_grad = side_grad[:, maps : maps + heads]
    block_out = (resid + own_out.astype(F32)).astype(BF)
    scaled = d_normed * in_gain
    in_grad = (
        cotangent.astype(F32) + scaled * in_scale
        - resid * in_scale**3 * jnp.sum(scaled * resid, axis=-1, keepdims=True) / model
    )
    in_gain_part = jnp.sum(d_normed * resid * in_scale, axis=0)
    over_head = lax.psum(
        (jnp.concatenate([gcs.reshape(-1), in_gain_part]), side_grad[:, :maps]), "head")
    state_proj_grad = over_head[1]
    packed = lax.psum(jnp.concatenate([over_head[0], gcv.reshape(-1), gh.reshape(-1), og[0]]), "dp")
    at = 8 * maps
    gcs = packed[:at].reshape(8, maps)
    in_gain_grad = packed[at : at + model]
    at = at + model
    gcv = packed[at : at + 8 * chans].reshape(8, chans)
    at = at + 8 * chans
    gh = packed[at : at + 8 * LANES].reshape(8, LANES)
    og = packed[at + 8 * LANES :]
    return (
        block_out, in_grad, in_gain_grad, gate_proj_grad, value_proj_grad, state_proj_grad, step_proj_grad,
        gcv[:taps_n], gcv[4], gcs[:taps_n], gcs[4], gh[0, :heads], gh[1, :heads], gh[2, :heads], og, out_proj_grad,
    )


def solution(mesh):
    placed = (
        P(("dp", "head"), None),
        P(),
        P(None, "head"),
        P(None, "head"),
        P(),
        P(None, "head"),
        P(None, "head"),
        P("head"),
        P(),
        P(),
        P("head"),
        P("head"),
        P("head"),
        P("head"),
        P("head", None),
        P(("dp", "head"), None),
        P("dp"),
    )
    return jax.shard_map(
        per_device,
        mesh=mesh,
        in_specs=placed,
        out_specs=(
            P(("dp", "head"), None),
            P(("dp", "head"), None),
            P(),
            P("dp", "head"),
            P("dp", "head"),
            P("dp", None),
            P("dp", "head"),
            P(None, "head"),
            P("head"),
            P(),
            P(),
            P("head"),
            P("head"),
            P("head"),
            P("head"),
            P("head", "dp"),
        ),
        check_vma=False,
    )
```

time: 1200 us -> 638 us (0.53)
  waiting for transfers between devices: 588 us -> 386 us
  matrix products: 239 us -> 77.9 us
  local copies, waits for them, and re-layouts: 109 us -> 23.7 us
  other arithmetic: 101 us -> 16.5 us
  blocking collectives: 128 us -> 56 us
  Pallas kernels: 0 us -> 51.7 us
    reduce_scatter x7 -> x6, waiting for transfers between devices: 553 us -> 318 us  [the longest x1 89.5 us: per_device(): lax.psum_scatter(t_mm(whole, d_value).astype(BF), 'dp', scatter_dimension...]
    dot_general x28 -> x12, matrix products: 239 us -> 77.9 us  [the longest x4 30.9 us: t_mm(): lax.dot_general(a, b, (((0,), (0,)), ((), ())), preferred_element_type=F32)]
    reshape x16 -> x0, local copies, waits for them, and re-layouts: 88.7 us -> none  [the longest x4 31.4 us: mix_block(): return result.reshape(seq_len, -1) * jax.nn.silu(gate_pre)]
    psum x5 -> x3, blocking collectives: 128 us -> 56 us  [the longest x1 39.7 us: per_device(): lax.psum(jnp.concatenate([over_head[0], gcv.reshape(-1), gh.reshape(-1),...]
    pallas_call x0 -> x4, Pallas kernels: none -> 51.7 us  [the longest x1 31 us: scan_bwd(): pl.pallas_call(functools.partial(bwd_kernel, span, heads, taps_n), grid=(...]
    psum x0 -> x1, waiting for transfers between devices: none -> 30.5 us  [per_device(): lax.psum((jnp.concatenate([gcs.reshape(-1), in_gain_part]), side_grad[:,...]
    reduce_sum x11 -> x1, other arithmetic: 29.7 us -> 1.98 us  [per_device(): in_gain_part = jnp.sum(d_normed * resid * in_scale, axis=0)]
    mul x6 -> x0, other arithmetic: 13.2 us -> none  [the longest x2 5.82 us: conv_causal(): running = running + kernel[offset][None, :] * padded[offset:offset + length]]
  transfers between devices with their start and end apart: 9 -> 9, of which waited for: 6 -> 9; matrix products, arithmetic and copies ran while one was open for 18% -> 14% of each run, Pallas kernels for 0% -> 2%
where the time goes in v1:
time: 638 us; the launch traced here: 628 us
  waiting for transfers between devices  386 us (61%)
  matrix products  77.9 us (12%)
  blocking collectives  56 us (9%)
  Pallas kernels  51.7 us (8%)
  local copies, waits for them, and re-layouts  23.7 us (4%)
  other arithmetic  16.5 us (3%)
  between operations  15.1 us (2%)
    reduce_scatter x1, waiting for transfers between devices, per_device(): lax.psum_scatter(t_mm(whole, d_value).astype(BF), 'dp', scatter_dimension...  89.5 us
    reduce_scatter x1, waiting for transfers between devices, per_device(): lax.psum_scatter(t_mm(whole, d_gate).astype(BF), 'dp', scatter_dimension=...  89.2 us
    reduce_scatter x1, waiting for transfers between devices, per_device(): lax.psum_scatter(out_part, 'head', scatter_dimension=0, tiled=True)  44.9 us
    reduce_scatter x1, waiting for transfers between devices, per_device(): lax.psum_scatter(d_normed, 'head', scatter_dimension=0, tiled=True)  42.9 us
    psum x1, blocking collectives, per_device(): lax.psum(jnp.concatenate([over_head[0], gcv.reshape(-1), gh.reshape(-1),...  39.7 us
    reduce_scatter x1, waiting for transfers between devices, per_device(): lax.psum_scatter(t_mm(normed_out, cot_all).astype(BF), 'dp', scatter_dime...  38.9 us
    all_gather x1, waiting for transfers between devices, per_device(): whole = lax.all_gather(normed, 'head', axis=0, tiled=True)  34.7 us
    pallas_call x1, Pallas kernels, scan_bwd(): pl.pallas_call(functools.partial(bwd_kernel, span, heads, taps_n), grid=(...  31 us
  transfers between devices with their start and end apart: 9, of which 9 were waited for; matrix products, arithmetic and copies ran while one was open for 14% of the time, Pallas kernels for 2%

profile of v1, /device:TPU:0, one launch (start us, length us, event | category | flops | bytes accessed | tf_op | source)
XLA Modules:
  0.0 628.2 jit_solution(1484480503182851700)
XLA Ops:
  7.3 1.5 fusion.3
  8.9 2.5 fusion.5
  11.4 0.7 all-gather.5.cloned.1.call-update
  14.0 34.7 %all-gather.3.cloned.1.call-done = bf16[1024,2048]{1,0:T(8,128)(2,1)} async-done(((bf16[256,2048]{1,0:T(8,128)(2,1)}), bf16[1024,2048]{1,0:T(8,128)(2,1)}) %all-gather.3.cloned.1.call-update) | async-done | bytes 4194320 | tf_op jit(solution)/shard_map/all_gather | solution.py:452
  48.7 5.0 fusion.12.ss_ref.sh_ref
  53.8 4.5 fusion.22.vp_ref.vh_ref
  58.3 12.4 %scan_fwd.1 = (f32[1024,1024]{1,0:T(8,128)S(1)}, bf16[8,128,1024]{2,1,0:T(8,128)(2,1)S(1)}) custom-call(f32[1024,1024]{1,0:T(8,128)S(1)} %fusion.22.vp_ref.vh_ref, f32[1024,384]{1,0:T(8,128)S(1)} %fusion.12.ss_ref.sh_ref, f32[8,1024]{1,0:T(8,128)S(1)} %concatenate.19.cv_ref, f32[8,256]{1,0:T(8,128)S(1)} %maximum_maximum_fusion.3.cs_ref, ...), custom_call_target="tpu_custom_call" | custom-call | tf_op jit(solution)/shard_map/scan_fwd/pallas_call | solution.py:276
  70.7 2.0 copy-done
  72.7 1.9 copy-done.1
  74.7 1.4 copy-done.6
  76.0 6.1 fusion.23.gate_ref
  82.1 2.7 all-gather.5.cloned.1.call-done
  84.8 7.7 %fusion.24.dno_ref = f32[1024,1024]{1,0:T(8,128)S(1)} fusion(bf16[1024,2048]{1,0:T(8,128)(2,1)} %all-gather.5.cloned.1.call-done, bf16[1024,2048]{1,0:T(8,128)(2,1)} %param.31), kind=kOutput, calls=%fused_computation.58 | convolution fusion | flops 4294967296 | bytes 12582912 | tf_op jit(solution)/shard_map/dot_general | solution.py:20
  92.6 1.9 row_sums.1
  94.6 6.2 psum.28
  100.8 2.2 copy-done.3
  103.0 6.4 %norm_both.1 = (bf16[1024,1024]{1,0:T(8,128)(2,1)S(1)}, bf16[1024,1024]{1,0:T(8,128)(2,1)S(1)}, bf16[1024,1024]{1,0:T(8,128)(2,1)S(1)}, f32[8,1024]{1,0:T(8,128)S(1)}) custom-call(f32[1024,1024]{1,0:T(8,128)S(1)} %copy-done.3, f32[1024,1024]{1,0:T(8,128)} %fusion.23.gate_ref, f32[1024,1024]{1,0:T(8,128)} %copy-done.5, f32[8,1024]{1,0:T(8,128)S(1)} %concatenate.19.cv_ref, ...), custom_call_target="tpu_custom_call" | custom-call | tf_op jit(solution)/shard_map/norm_both/pallas_call | solution.py:419
  109.4 1.3 copy-done.7
  110.7 1.3 copy-done.8
  112.0 1.3 copy-done.10
  113.3 31.0 %scan_bwd.1 = (bf16[1024,1024]{1,0:T(8,128)(2,1)S(1)}, bf16[1024,384]{1,0:T(8,128)(2,1)S(1)}, f32[8,1024]{1,0:T(8,128)S(1)}, f32[8,256]{1,0:T(8,128)S(1)}, f32[8,128]{1,0:T(8,128)S(1)}) custom-call(f32[1024,1024]{1,0:T(8,128)} %copy-done, f32[1024,1024]{1,0:T(8,128)} %copy-done, f32[1024,384]{1,0:T(8,128)S(1)} %fusion.12.ss_ref.sh_ref, ...), custom_call_target="tpu_custom_call" | custom-call | tf_op jit(solution)/shard_map/scan_bwd/pallas_call | solution.py:311
  144.3 1.3 copy-done.12
  145.7 3.6 convolution_convert_fusion.4
  149.8 6.5 %fusion.25 = f32[1024,2048]{1,0:T(8,128)S(1)} fusion(bf16[1024,1024]{1,0:T(8,128)(2,1)S(1)} %copy-done.11, bf16[2048,1024]{1,0:T(8,128)(2,1)} %param.19), kind=kOutput, calls=%fused_computation.59 | convolution fusion | flops 4294967296 | bytes 14680064 | tf_op jit(solution)/shard_map/dot_general | solution.py:20
  156.3 4.6 fusion.26
  160.9 4.4 add_convert_fusion
  165.3 1.5 copy-done.9
  166.9 8.4 %convolution_convert_fusion = bf16[1024,2048]{1,0:T(8,128)(2,1)} fusion(bf16[1024,1024]{1,0:T(8,128)(2,1)S(1)} %copy-done.9, bf16[1024,2048]{1,0:T(8,128)(2,1)} %all-gather.5.cloned.1.call-done), kind=kOutput, calls=%fused_computation.7 | convolution fusion | flops 4297064448 | bytes 10485760 | tf_op jit(solution)/shard_map/dot_general | solution.py:24
  175.5 9.5 %convolution_convert_fusion.1 = bf16[2048,1024]{1,0:T(8,128)(2,1)} fusion(bf16[1024,2048]{1,0:T(8,128)(2,1)} %all-gather.3.cloned.1.call-done, bf16[1024,1024]{1,0:T(8,128)(2,1)} %copy-done.12), kind=kOutput, calls=%fused_computation.8 | convolution fusion | flops 4297064448 | bytes 10485760 | tf_op jit(solution)/shard_map/dot_general | solution.py:24
  185.1 9.4 %convolution_convert_fusion.2 = bf16[2048,1024]{1,0:T(8,128)(2,1)} fusion(bf16[1024,2048]{1,0:T(8,128)(2,1)} %all-gather.3.cloned.1.call-done, bf16[1024,1024]{1,0:T(8,128)(2,1)} %copy-done.10), kind=kOutput, calls=%fused_computation.9 | convolution fusion | flops 4297064448 | bytes 10485760 | tf_op jit(solution)/shard_map/dot_general | solution.py:24
  194.6 8.3 %convolution_convert_fusion.3 = bf16[1024,2048]{1,0:T(8,128)(2,1)} fusion(bf16[1024,1024]{1,0:T(8,128)(2,1)S(1)} %copy-done.9, bf16[1024,2048]{1,0:T(8,128)(2,1)} %param.31), kind=kOutput, calls=%fused_computation.10 | convolution fusion | flops 4297064448 | bytes 10485760 | tf_op jit(solution)/shard_map/dot_general | solution.py:16
  203.0 12.3 %reduce-scatter.15.cloned.1.call-done = bf16[256,384]{1,0:T(8,128)(2,1)} async-done(((bf16[2048,384]{1,0:T(8,128)(2,1)}), bf16[256,384]{1,0:T(8,128)(2,1)}) %reduce-scatter.15.cloned.1.call-update) | async-done | bytes 196624 | tf_op jit(solution)/shard_map/reduce_scatter | solution.py:483
  215.3 0.8 slice.106
  216.8 1.6 slice.105
  218.5 42.9 %reduce-scatter.9.cloned.1.call-done = bf16[256,2048]{1,0:T(8,128)(2,1)} async-done(((bf16[1024,2048]{1,0:T(8,128)(2,1)}), bf16[256,2048]{1,0:T(8,128)(2,1)}) %reduce-scatter.9.cloned.1.call-update) | async-done | bytes 1048592 | tf_op jit(solution)/shard_map/reduce_scatter | solution.py:482
  261.4 2.0 fusion.11
  263.4 10.1 %psum.29 = f32[4096]{0:T(1024)S(1)} all-reduce(f32[4096]{0:T(1024)S(1)} %pad_maximum_fusion.1), channel_id=1, replica_groups=mesh['dp'=8,'head'=4] {'head'}, use_global_device_ids=true, to_apply=%region_6.7 | all-reduce | flops 4096 | bytes 32768 | tf_op jit(solution)/shard_map/psum | solution.py:493
  273.5 39.7 %psum.30 = f32[14336]{0:T(1024)S(1)} all-reduce(f32[14336]{0:T(1024)S(1)} %pad_maximum_fusion), channel_id=1, replica_groups=mesh['dp'=8,'head'=4] {'dp'}, use_global_device_ids=true, to_apply=%region_7.8 | all-reduce | flops 14336 | bytes 114688 | tf_op jit(solution)/shard_map/psum | solution.py:496
  316.1 38.9 %reduce-scatter.17.cloned.1.call-done = bf16[1024,256]{1,0:T(8,128)(2,1)} async-done(((bf16[1024,2048]{1,0:T(8,128)(2,1)}), bf16[1024,256]{1,0:T(8,128)(2,1)}) %reduce-scatter.17.cloned.1.call-update) | async-done | bytes 524304 | tf_op jit(solution)/shard_map/reduce_scatter | solution.py:473
  355.0 2.1 convert_element_type.82
  357.1 89.5 %reduce-scatter.13.cloned.1.call-done = bf16[256,1024]{1,0:T(8,128)(2,1)} async-done(((bf16[2048,1024]{1,0:T(8,128)(2,1)}), bf16[256,1024]{1,0:T(8,128)(2,1)}) %reduce-scatter.13.cloned.1.call-update) | async-done | bytes 524304 | tf_op jit(solution)/shard_map/reduce_scatter | solution.py:479
  446.6 2.1 convert_element_type.78
  448.7 89.2 %reduce-scatter.11.cloned.1.call-done = bf16[256,1024]{1,0:T(8,128)(2,1)} async-done(((bf16[2048,1024]{1,0:T(8,128)(2,1)}), bf16[256,1024]{1,0:T(8,128)(2,1)}) %reduce-scatter.11.cloned.1.call-update) | async-done | bytes 524304 | tf_op jit(solution)/shard_map/reduce_scatter | solution.py:475
  537.9 2.1 convert_element_type.76
  540.0 44.9 %reduce-scatter.7.cloned.1.call-done = bf16[256,2048]{1,0:T(8,128)(2,1)} async-done(((bf16[1024,2048]{1,0:T(8,128)(2,1)}), bf16[256,2048]{1,0:T(8,128)(2,1)}) %reduce-scatter.7.cloned.1.call-update) | async-done | bytes 1048592 | tf_op jit(solution)/shard_map/reduce_scatter | solution.py:472
  584.9 3.9 fusion.2
  589.3 30.5 %all-reduce.5.cloned.1.call-done = f32[256,256]{1,0:T(8,128)} async-done(((f32[256,256]{1,0:T(8,128)}), f32[256,256]{1,0:T(8,128)}) %all-reduce.5.cloned.1.call-update) | async-done | bytes 262160 | tf_op jit(solution)/shard_map/psum | solution.py:493
  619.8 1.7 copy.41
  (110 shorter events, 6.6 us)
Async XLA Ops:
  7.2 6.0 copy-start.25
  7.2 6.1 copy-start.19
  7.2 6.5 %copy-start.22 = (f32[1024]{0:T(1024)S(1)}, f32[1024]{0:T(1024)}, u32[]{:S(2)}) copy-start(f32[1024]{0:T(1024)} %param.30) | copy-start | bytes 12292
  7.2 6.5 %copy-start.21 = (f32[1024]{0:T(1024)S(1)}, f32[1024]{0:T(1024)}, u32[]{:S(2)}) copy-start(f32[1024]{0:T(1024)} %param.24) | copy-start | bytes 12292
  7.2 6.5 %copy-start.20 = (f32[4,1024]{1,0:T(4,128)S(1)}, f32[4,1024]{1,0:T(4,128)}, u32[]{:S(2)}) copy-start(f32[4,1024]{1,0:T(4,128)} %param.23) | copy-start | bytes 49156
  7.2 6.5 %copy-start.32 = (f32[16]{0:T(128)S(1)}, f32[16]{0:T(128)}, u32[]{:S(2)}) copy-start(f32[16]{0:T(128)} %param.28) | copy-start | bytes 196
  7.2 6.5 %copy-start.26 = (f32[16]{0:T(128)S(1)}, f32[16]{0:T(128)}, u32[]{:S(2)}) copy-start(f32[16]{0:T(128)} %param.27) | copy-start | bytes 196
  7.3 6.6 %copy-start.24 = (f32[256]{0:T(256)S(1)}, f32[256]{0:T(256)}, u32[]{:S(2)}) copy-start(f32[256]{0:T(256)} %param.26) | copy-start | bytes 3076
  7.3 6.6 %copy-start.23 = (f32[4,256]{1,0:T(4,128)S(1)}, f32[4,256]{1,0:T(4,128)}, u32[]{:S(2)}) copy-start(f32[4,256]{1,0:T(4,128)} %param.25) | copy-start | bytes 12292
  7.3 41.5 %all-gather.3.cloned.1.call-start = ((), (), s32[]{:S(2)}) async-start(), calls=%async_computation.6 | async-start | bytes 5242880 | tf_op jit(solution)/shard_map/all_gather | solution.py:452
  11.4 73.4 %all-gather.5.cloned.1.call-start = ((), (), s32[]{:S(2)}) async-start(), calls=%async_computation.7 | async-start | bytes 5242880 | tf_op jit(solution)/shard_map/all_gather | solution.py:453
  12.1 203.1 %reduce-scatter.15.cloned.1.call-start = ((), (), s32[]{:S(2)}) async-start(), calls=%async_computation.12 | async-start | bytes 1769472 | tf_op jit(solution)/shard_map/reduce_scatter | solution.py:483
  48.7 5.0 copy-start.28
  48.7 5.0 copy-start.30
  58.3 17.7 %copy-start.27 = (bf16[2048,1024]{1,0:T(8,128)(2,1)S(1)}, bf16[2048,1024]{1,0:T(8,128)(2,1)}, u32[]{:S(2)}) copy-start(bf16[2048,1024]{1,0:T(8,128)(2,1)} %param.19) | copy-start | bytes 12582916
  70.7 2.0 copy-start
  72.7 1.9 copy-start.1
  74.6 1.4 copy-start.6
  84.8 7.8 %copy-start.2 = (f32[1024,1024]{1,0:T(8,128)S(1)}, f32[1024,1024]{1,0:T(8,128)}, u32[]{:S(2)}) copy-start(f32[1024,1024]{1,0:T(8,128)} %copy-done.1) | copy-start | bytes 12582916
  84.8 7.8 %copy-start.4 = (f32[1024,1024]{1,0:T(8,128)S(1)}, f32[1024,1024]{1,0:T(8,128)}, u32[]{:S(2)}) copy-start(f32[1024,1024]{1,0:T(8,128)} %fusion.23.gate_ref) | copy-start | bytes 12582916
  92.5 2.0 copy-start.5
  100.8 2.2 copy-start.3
  109.3 1.3 copy-start.7
  110.7 1.3 copy-start.8
  112.0 1.3 copy-start.10
  113.3 32.4 %copy-start.31 = (bf16[1024,2048]{1,0:T(8,128)(2,1)S(1)}, bf16[1024,2048]{1,0:T(8,128)(2,1)}, u32[]{:S(2)}) copy-start(bf16[1024,2048]{1,0:T(8,128)(2,1)} %all-gather.3.cloned.1.call-done) | copy-start | bytes 12582916
  144.3 1.3 copy-start.12
  145.7 4.1 copy-start.11
  149.3 112.1 %reduce-scatter.9.cloned.1.call-start = ((), (), s32[]{:S(2)}) async-start(), calls=%async_computation.9 | async-start | bytes 5242880 | tf_op jit(solution)/shard_map/reduce_scatter | solution.py:482
  149.7 6.6 %copy-start.13 = (bf16[1024,1024]{1,0:T(8,128)(2,1)S(1)}, bf16[1024,1024]{1,0:T(8,128)(2,1)}, u32[]{:S(2)}) copy-start(bf16[1024,1024]{1,0:T(8,128)(2,1)} %copy-done.12) | copy-start | bytes 6291460
  149.8 6.6 %copy-start.29 = (bf16[2048,1024]{1,0:T(8,128)(2,1)S(1)}, bf16[2048,1024]{1,0:T(8,128)(2,1)}, u32[]{:S(2)}) copy-start(bf16[2048,1024]{1,0:T(8,128)(2,1)} %param.20) | copy-start | bytes 12582916
  156.3 4.6 copy-start.17
  165.3 1.6 copy-start.9
  165.3 189.7 %reduce-scatter.17.cloned.1.call-start = ((), (), s32[]{:S(2)}) async-start(), calls=%async_computation.14 | async-start | bytes 4718592 | tf_op jit(solution)/shard_map/reduce_scatter | solution.py:473
  175.3 271.3 %reduce-scatter.13.cloned.1.call-start = ((), (), s32[]{:S(2)}) async-start(), calls=%async_computation.11 | async-start | bytes 4718592 | tf_op jit(solution)/shard_map/reduce_scatter | solution.py:479
  185.0 352.9 %reduce-scatter.11.cloned.1.call-start = ((), (), s32[]{:S(2)}) async-start(), calls=%async_computation.10 | async-start | bytes 4718592 | tf_op jit(solution)/shard_map/reduce_scatter | solution.py:475
  194.5 390.4 %reduce-scatter.7.cloned.1.call-start = ((), (), s32[]{:S(2)}) async-start(), calls=%async_computation.8 | async-start | bytes 5242880 | tf_op jit(solution)/shard_map/reduce_scatter | solution.py:472
  202.8 58.5 %copy-start.14 = (bf16[256,2048]{1,0:T(8,128)(2,1)S(1)}, bf16[256,2048]{1,0:T(8,128)(2,1)}, u32[]{:S(2)}) copy-start(bf16[256,2048]{1,0:T(8,128)(2,1)} %param.17) | copy-start | bytes 3145732
  202.8 58.5 %copy-start.18 = (f32[2048]{0:T(1024)S(1)}, f32[2048]{0:T(1024)}, u32[]{:S(2)}) copy-start(f32[2048]{0:T(1024)} %param.18) | copy-start | bytes 24580
  202.9 416.9 %all-reduce.5.cloned.1.call-start = ((), (), s32[]{:S(2)}) async-start(), calls=%async_computation.13 | async-start | bytes 524288 | tf_op jit(solution)/shard_map/psum | solution.py:493
  218.5 366.4 %copy-start.16 = (bf16[256,2048]{1,0:T(8,128)(2,1)S(1)}, bf16[256,2048]{1,0:T(8,128)(2,1)}, u32[]{:S(2)}) copy-start(bf16[256,2048]{1,0:T(8,128)(2,1)} %param.32) | copy-start | bytes 3145732
  261.4 323.5 %copy-start.15 = (bf16[256,2048]{1,0:T(8,128)(2,1)S(1)}, bf16[256,2048]{1,0:T(8,128)(2,1)}, u32[]{:S(2)}) copy-start(bf16[256,2048]{1,0:T(8,128)(2,1)} %reduce-scatter.9.cloned.1.call-done) | copy-start | bytes 3145732
Sparse Core Ops, SparseCore 0:
  11.5 37.1 all-gather.2
  50.3 34.4 all-gather.4
  149.4 65.8 reduce-scatter.14
  217.8 43.4 reduce-scatter.8
  264.8 90.1 reduce-scatter.16
  358.9 87.6 reduce-scatter.12
  450.2 87.6 reduce-scatter.10
  540.6 44.2 reduce-scatter.6
  587.8 31.9 all-reduce.4

commit v2 on v1

--- a/solution.py
+++ b/solution.py
@@ -432,6 +432,310 @@
     )(ssd, gate, dno, cv, sums, count)
 
 
+MESH = pl.DeviceIdType.MESH
+
+
+def remote(src, dst, sems, at, device):
+    return pltpu.make_async_remote_copy(
+        src_ref=src, dst_ref=dst, send_sem=sems.at[0, at], recv_sem=sems.at[1, at],
+        device_id=device, device_id_type=MESH)
+
+
+def greet(devices):
+    barrier = pltpu.get_barrier_semaphore()
+    for device in devices:
+        pl.semaphore_signal(barrier, inc=1, device_id=device, device_id_type=MESH)
+    pl.semaphore_wait(barrier, len(devices))
+
+
+def chunks(rows, size, body):
+    def step(i, carry):
+        body(pl.ds(pl.multiple_of(i * size, size), size))
+        return carry
+
+    lax.fori_loop(0, rows // size, step, 0)
+
+
+class RingSum:
+    def __init__(self, parts, slots, sems, dp, head):
+        self.parts, self.slots, self.sems = parts, slots, sems
+        z, x = dp // 2, lax.rem(dp, 2)
+        self.place = z * (1 - x) + (7 - z) * x
+        self.head = head
+        self.half = slots.shape[2]
+        self.sent = []
+
+    def block(self, shift):
+        at = lax.rem(self.place + shift + 16, 8)
+        x = at // 4
+        return (at * (1 - x) + (7 - at) * x) * 2 + x
+
+    def send(self, hop):
+        for way in range(2):
+            sign = 1 - 2 * way
+            if hop == 0:
+                source = self.parts.at[self.block(-sign), pl.ds(way * self.half, self.half)]
+            else:
+                source = self.slots.at[way, hop - 1]
+            copy = pltpu.make_async_remote_copy(
+                src_ref=source, dst_ref=self.slots.at[way, hop],
+                send_sem=self.sems.at[0, way, hop], recv_sem=self.sems.at[1, way, hop],
+                device_id=(self.block(sign), self.head), device_id_type=MESH)
+            copy.start()
+            self.sent.append(copy)
+
+    def start(self):
+        self.send(0)
+
+    def step(self, hop):
+        for way in range(2):
+            self.sent[2 * hop + way].wait_recv()
+            block = self.block((2 * way - 1) * (2 + hop))
+
+            def add(rows):
+                low = pl.ds(pl.multiple_of(rows.start + way * self.half, 32), 32)
+                self.slots[way, hop, rows, :] = (
+                    self.slots[way, hop, rows, :].astype(F32) + self.parts[block, low, :].astype(F32)).astype(BF)
+
+            chunks(self.half, 32, add)
+        self.send(hop + 1)
+
+    def finish(self, emit):
+        mine = self.block(0)
+        for way in range(2):
+            self.sent[12 + way].wait_recv()
+
+            def add(rows):
+                low = pl.ds(pl.multiple_of(rows.start + way * self.half, 32), 32)
+                emit(low, self.slots[way, 6, rows, :].astype(F32) + self.parts[mine, low, :].astype(F32))
+
+            chunks(self.half, 32, add)
+        for copy in self.sent:
+            copy.wait_send()
+
+
+class OverHead:
+    def __init__(self, source, local, got, total, got2, sems, copy_sem, place):
+        self.source, self.local, self.got, self.total, self.got2, self.sems = source, local, got, total, got2, sems
+        self.y, self.core, self.over_core, self.over_y = place
+        self.keep = pltpu.make_async_copy(source.at[:, self.core], local, copy_sem)
+
+    def start(self):
+        self.copies = []
+        for i in range(2):
+            row = lax.rem(self.y + 1 + i, 2)
+            copy = remote(self.source.at[row, 1 - self.core], self.got.at[i], self.sems, i, self.over_core)
+            copy.start()
+            self.copies.append(copy)
+        self.keep.start()
+
+    def middle(self):
+        self.keep.wait()
+        self.copies[0].wait_recv()
+        rows_n = self.got2.shape[0]
+        parts = 4
+        size = rows_n // parts
+        self.cross = []
+        for part in range(parts):
+            def add(rows):
+                at = pl.ds(pl.multiple_of(part * size + rows.start, 16), 16)
+                self.total[at, :] = (
+                    self.local[1 - self.y, at, :].astype(F32) + self.got[0, at, :].astype(F32)).astype(BF)
+
+            chunks(size, 16, add)
+            at = pl.ds(part * size, size)
+            copy = remote(self.total.at[at], self.got2.at[at], self.sems, 2 + part, self.over_y)
+            copy.start()
+            self.cross.append(copy)
+
+    def finish(self, emit):
+        self.copies[1].wait_recv()
+        for copy in self.cross:
+            copy.wait_recv()
+
+        def add(rows):
+            emit(rows, self.local[self.y, rows, :].astype(F32) + self.got[1, rows, :].astype(F32)
+                 + self.got2[rows, :].astype(F32))
+
+        chunks(self.got2.shape[0], 16, add)
+        for copy in (*self.copies, *self.cross):
+            copy.wait_send()
+
+
+def places():
+    dp, head = lax.axis_index("dp"), lax.axis_index("head")
+    y, core = head // 2, lax.rem(head, 2)
+    over_core = (dp, y * 2 + 1 - core)
+    over_y = (dp, (1 - y) * 2 + core)
+    return dp, head, (y, core, over_core, over_y)
+
+
+def closing_kernel(
+    model, maps,
+    go_ref, gg_ref, gv_ref, gs_ref, op_ref, dn_ref, hid_ref, cot_ref, gain_ref, gcv_ref, og_ref, gh_ref, gcs_ref,
+    block_ref, ingrad_ref, og_out, gg_out, gv_out, gs_out, small1, small2,
+    *scratch,
+):
+    (slots_o, sems_o, slots_g, sems_g, slots_v, sems_v, slots_s, sems_d) = scratch[:8]
+    heads_set = [scratch[8 + 4 * i : 12 + 4 * i] for i in range(2)]
+    (copy_sems, sems_h0, sems_h1, small_in1, small_in2, got_s2, got_s1b, got_s2b, state_own, got_state,
+     sems_s, ig_acc) = scratch[16:]
+    dp, head, head_place = places()
+    peers_head = [(dp, lax.rem(head + k, 4)) for k in range(1, 4)]
+    peers_dp = [(lax.rem(dp + k, 8), head) for k in range(1, 8)]
+    greet(peers_head + peers_dp)
+
+    out_w = RingSum(go_ref, slots_o, sems_o, dp, head)
+    gate_w = RingSum(gg_ref, slots_g, sems_g, dp, head)
+    value_w = RingSum(gv_ref, slots_v, sems_v, dp, head)
+    side_w = RingSum(gs_ref, slots_s, sems_d, dp, head)
+    d_normed = OverHead(dn_ref, *heads_set[0], sems_h0, copy_sems.at[0], head_place)
+    own_out = OverHead(op_ref, *heads_set[1], sems_h1, copy_sems.at[1], head_place)
+    d_normed.start()
+    side_w.start()
+    out_w.start()
+    gate_w.start()
+    value_w.start()
+    own_out.start()
+    d_normed.middle()
+    for hop in range(6):
+        side_w.step(hop)
+        out_w.step(hop)
+        if hop == 0:
+            own_out.middle()
+        gate_w.step(hop)
+        value_w.step(hop)
+
+    def give_state(rows, value):
+        gs_out[rows, :] = value
+
+    side_w.finish(give_state)
+    state_own[...] = gs_out[:, :maps].astype(BF)
+    state_copies = []
+    for k, peer in enumerate(peers_head):
+        copy = remote(state_own, got_state.at[k], sems_s, k, peer)
+        copy.start()
+        state_copies.append(copy)
+
+    ig_acc[...] = jnp.zeros_like(ig_acc)
+
+    def give_in(rows, d_n):
+        resid = hid_ref[rows, :].astype(F32)
+        scale = lax.rsqrt(jnp.mean(resid * resid, axis=-1, keepdims=True) + EPS)
+        scaled = d_n * gain_ref[...]
+        ingrad_ref[rows, :] = (
+            cot_ref[rows, :].astype(F32) + scaled * scale
+            - resid * (scale * scale * scale * (jnp.sum(scaled * resid, axis=-1, keepdims=True) / model)))
+        ig_acc[0:1, :] = ig_acc[0:1, :] + jnp.sum(d_n * resid * scale, axis=0, keepdims=True)
+
+    d_normed.finish(give_in)
+    wide = small_in2.shape[1]
+    small_in2[...] = jnp.zeros_like(small_in2)
+    for i in range(model // wide):
+        small_in2[i : i + 1, :] = ig_acc[0:1, i * wide : (i + 1) * wide]
+    per = wide // maps
+    for k in range(5):
+        row = model // wide + k // per
+        lanes = slice((k % per) * maps, (k % per + 1) * maps)
+        small_in2[row : row + 1, lanes] = gcs_ref[k : k + 1, :]
+    small_in1[...] = gcv_ref[...]
+    small_in1[5:6, :] = og_ref[0:1, :]
+    for k in range(3):
+        small_in1[6:7, k * LANES : (k + 1) * LANES] = gh_ref[k : k + 1, :]
+    first = []
+    for k, peer in enumerate(peers_head):
+        copy = remote(small_in2, got_s2.at[k], sems_s, 3 + k, peer)
+        copy.start()
+        first.append(copy)
+    second = []
+    for k, peer in enumerate(peers_dp):
+        copy = remote(small_in1, got_s1b.at[k], sems_s, 6 + k, peer)
+        copy.start()
+        second.append(copy)
+    for copy in first:
+        copy.wait_recv()
+    small2[...] = small_in2[...] + got_s2[0] + got_s2[1] + got_s2[2]
+    third = []
+    for k, peer in enumerate(peers_dp):
+        copy = remote(small2, got_s2b.at[k], sems_s, 13 + k, peer)
+        copy.start()
+        third.append(copy)
+
+    def give_out(rows, value):
+        block_ref[rows, :] = (hid_ref[rows, :].astype(F32) + value).astype(BF)
+
+    own_out.finish(give_out)
+
+    def give(ref):
+        def emit(rows, value):
+            ref[rows, :] = value
+        return emit
+
+    out_w.finish(give(og_out))
+    gate_w.finish(give(gg_out))
+    for copy in state_copies:
+        copy.wait_recv()
+    gs_out[:, :maps] = gs_out[:, :maps] + got_state[0].astype(F32) + got_state[1].astype(F32) + got_state[2].astype(F32)
+    value_w.finish(give(gv_out))
+    for copy in (*second, *third):
+        copy.wait_recv()
+    for copy in third:
+        copy.wait_send()
+    total1, total2 = small_in1[...], small2[...]
+    for k in range(7):
+        total1 = total1 + got_s1b[k]
+        total2 = total2 + got_s2b[k]
+    small1[...] = total1
+    small2[...] = total2
+    for copy in (*first, *second, *state_copies):
+        copy.wait_send()
+
+
+def closing(go, gg, gv, gs, op, dn, hidden, cot, in_gain, gcv, og, gh, gcs):
+    model = hidden.shape[1]
+    maps = gcs.shape[1]
+    rows = hidden.shape[0]
+    block = go.shape[1:]
+    side = gs.shape[1:]
+    anyspace = pl.BlockSpec(memory_space=pl.ANY)
+    vmem = pl.BlockSpec(memory_space=pltpu.VMEM)
+    sem = pltpu.SemaphoreType.DMA
+
+    def head_set():
+        return [
+            pltpu.VMEM((2, rows, model), BF), pltpu.VMEM((2, rows, model), BF),
+            pltpu.VMEM((rows, model), BF), pltpu.VMEM((rows, model), BF),
+        ]
+
+    scratch = []
+    for shape in (block, block, block, side):
+        scratch += [pltpu.VMEM((2, 7, shape[0] // 2, shape[1]), BF), sem((2, 2, 7))]
+    for _ in range(2):
+        scratch += head_set()
+    small = pltpu.VMEM((8, 1024), F32)
+    extra = [
+        sem((2,)), sem((2, 6)), sem((2, 6)), small, small,
+        pltpu.VMEM((3, 8, 1024), F32), pltpu.VMEM((7, 8, 1024), F32), pltpu.VMEM((7, 8, 1024), F32),
+        pltpu.VMEM((rows, maps), BF), pltpu.VMEM((3, rows, maps), BF), sem((2, 20)),
+        pltpu.VMEM((8, model), F32),
+    ]
+    return pl.pallas_call(
+        functools.partial(closing_kernel, model, maps),
+        in_specs=[vmem] * 4 + [anyspace] * 2 + [vmem] * 7,
+        out_specs=[vmem] * 8,
+        out_shape=[
+            jax.ShapeDtypeStruct((rows, model), BF), jax.ShapeDtypeStruct((rows, model), F32),
+            jax.ShapeDtypeStruct(block, F32), jax.ShapeDtypeStruct(block, F32),
+            jax.ShapeDtypeStruct(block, F32), jax.ShapeDtypeStruct(side, F32),
+            jax.ShapeDtypeStruct((8, 1024), F32), jax.ShapeDtypeStruct((8, 1024), F32),
+        ],
+        scratch_shapes=scratch + extra,
+        compiler_params=pltpu.CompilerParams(
+            collective_id=0, has_side_effects=True, vmem_limit_bytes=60 << 20),
+        name="closing",
+    )(go, gg, gv, gs, op, dn, hidden, cot, in_gain[None, :], gcv, og, gh, gcs)
+
+
 def per_device(
     hidden_in, in_gain, gate_proj, value_proj, state_proj, step_proj, conv_value, conv_value_bias,
     conv_state, conv_state_bias, step_bias, decay_log, skip_gain, out_gain, out_proj, cotangent, width_level,
@@ -469,39 +773,42 @@
     sums = jnp.pad(lax.psum(sums[:2], "head"), ((0, 6), (0, 0)))
     normed_out, dy, d_gate, og = norm_both(ssd, gate_pre, d_normed_out, cv, sums, count)
     out_part = mm(normed_out, out_proj).astype(BF)
-    own_out = lax.psum_scatter(out_part, "head", scatter_dimension=0, tiled=True)
-    out_proj_grad = lax.psum_scatter(
-        t_mm(normed_out, cot_all).astype(BF), "dp", scatter_dimension=1, tiled=True).astype(F32)
-    gate_proj_grad = lax.psum_scatter(
-        t_mm(whole, d_gate).astype(BF), "dp", scatter_dimension=0, tiled=True).astype(F32)
+    part_out = t_mm(cot_all, normed_out).astype(BF)
+    part_gate = t_mm(whole, d_gate).astype(BF)
     d_value, d_side, gcv, gcs, gh = scan_bwd(
         value_pre, side_pre, dy, entering, cv, cs, hv, ex, heads, taps_n, span)
-    value_proj_grad = lax.psum_scatter(
-        t_mm(whole, d_value).astype(BF), "dp", scatter_dimension=0, tiled=True).astype(F32)
+    part_value = t_mm(whole, d_value).astype(BF)
     d_normed = (mm_t(d_gate, gate_proj) + mm_t(d_value, value_proj) + mm_t(d_side, side_proj)).astype(BF)
-    d_normed = lax.psum_scatter(d_normed, "head", scatter_dimension=0, tiled=True).astype(F32)
-    side_grad = lax.psum_scatter(
-        t_mm(whole, d_side).astype(BF), "dp", scatter_dimension=0, tiled=True).astype(F32)
-    step_proj_grad = side_grad[:, maps : maps + heads]
-    block_out = (resid + own_out.astype(F32)).astype(BF)
-    scaled = d_normed * in_gain
-    in_grad = (
-        cotangent.astype(F32) + scaled * in_scale
-        - resid * in_scale**3 * jnp.sum(scaled * resid, axis=-1, keepdims=True) / model
-    )
-    in_gain_part = jnp.sum(d_normed * resid * in_scale, axis=0)
-    over_head = lax.psum(
-        (jnp.concatenate([gcs.reshape(-1), in_gain_part]), side_grad[:, :maps]), "head")
-    state_proj_grad = over_head[1]
-    packed = lax.psum(jnp.concatenate([over_head[0], gcv.reshape(-1), gh.reshape(-1), og[0]]), "dp")
-    at = 8 * maps
-    gcs = packed[:at].reshape(8, maps)
-    in_gain_grad = packed[at : at + model]
-    at = at + model
-    gcv = packed[at : at + 8 * chans].reshape(8, chans)
-    at = at + 8 * chans
-    gh = packed[at : at + 8 * LANES].reshape(8, LANES)
-    og = packed[at + 8 * LANES :]
+    part_side = t_mm(whole, d_side).astype(BF)
+    if lax.axis_size("dp") == 8 and groups == 4 and chans == 1024 and model == 2 * chans:
+        by_dp = lambda v: v.reshape(8, model // 8, v.shape[1])
+        by_head = lambda v: v.reshape(2, 2, v.shape[0] // 4, model)
+        (block_out, in_grad, out_proj_grad, gate_proj_grad, value_proj_grad, side_grad, small1, small2) = closing(
+            by_dp(part_out), by_dp(part_gate), by_dp(part_value), by_dp(part_side), by_head(out_part),
+            by_head(d_normed), hidden_in, cotangent, in_gain, gcv, og, gh, gcs)
+        out_proj_grad = out_proj_grad.T
+        state_proj_grad = side_grad[:, :maps]
+        step_proj_grad = side_grad[:, maps : maps + heads]
+        gcv, og = small1, small1[5]
+        gh = jnp.pad(small1[6, : 3 * LANES].reshape(3, LANES), ((0, 5), (0, 0)))
+        in_gain_grad = small2[: model // chans].reshape(model)
+        gcs = small2[model // chans : model // chans + 2].reshape(-1, maps)
+    else:
+        over_dp = lambda v: lax.psum_scatter(v, "dp", scatter_dimension=0, tiled=True).astype(F32)
+        over_head = lambda v: lax.psum_scatter(v, "head", scatter_dimension=0, tiled=True).astype(F32)
+        block_out = (resid + over_head(out_part)).astype(BF)
+        d_normed = over_head(d_normed)
+        scaled = d_normed * in_gain
+        in_grad = (
+            cotangent.astype(F32) + scaled * in_scale
+            - resid * in_scale**3 * jnp.sum(scaled * resid, axis=-1, keepdims=True) / model
+        )
+        out_proj_grad = over_dp(part_out).T
+        gate_proj_grad, value_proj_grad, side_grad = over_dp(part_gate), over_dp(part_value), over_dp(part_side)
+        step_proj_grad = side_grad[:, maps : maps + heads]
+        in_gain_grad, gcs, state_proj_grad = lax.psum(
+            (jnp.sum(d_normed * resid * in_scale, axis=0), gcs, side_grad[:, :maps]), "head")
+        in_gain_grad, gcs, gcv, gh, og = lax.psum((in_gain_grad, gcs, gcv, gh, og[0]), "dp")
     return (
         block_out, in_grad, in_gain_grad, gate_proj_grad, value_proj_grad, state_proj_grad, step_proj_grad,
         gcv[:taps_n], gcv[4], gcs[:taps_n], gcs[4], gh[0, :heads], gh[1, :heads], gh[2, :heads], og, out_proj_grad,

time: 638 us -> 402 us (0.63)
  waiting for transfers between devices: 386 us -> 38.4 us
  Pallas kernels: 51.7 us -> 211 us
  blocking collectives: 56 us -> 6.25 us
  local copies, waits for them, and re-layouts: 23.7 us -> 36.1 us
  other arithmetic: 16.5 us -> 4.34 us
  matrix products: 77.9 us -> 85.4 us
    reduce_scatter x6 -> x0, waiting for transfers between devices: 318 us -> none  [the longest x1 89.5 us: per_device(): lax.psum_scatter(t_mm(whole, d_value).astype(BF), 'dp', scatter_dimension...]
    pallas_call x0 -> x1, Pallas kernels: none -> 158 us  [closing(): pl.pallas_call(functools.partial(closing_kernel, model, maps), in_specs=[...]
    psum x2 -> x0, blocking collectives: 49.8 us -> none  [the longest x1 39.7 us: per_device(): lax.psum(jnp.concatenate([over_head[0], gcv.reshape(-1), gh.reshape(-1),...]
    psum x1 -> x0, waiting for transfers between devices: 30.5 us -> none  [per_device(): lax.psum((jnp.concatenate([gcs.reshape(-1), in_gain_part]), side_grad[:,...]
    dot_general x4, matrix products: 23.2 us -> 31.7 us  [mm_t(): lax.dot_general(a, b, (((1,), (1,)), ((), ())), preferred_element_type=F32)]
    convert_element_type x0 -> x1, local copies, waits for them, and re-layouts: none -> 6.5 us  [per_device(): part_out = t_mm(cot_all, normed_out).astype(BF)]
    unnamed x71 -> x84, local copies, waits for them, and re-layouts: 17.1 us -> 19.4 us
  transfers between devices with their start and end apart: 9 -> 2, of which waited for: 9 -> 2; matrix products, arithmetic and copies ran while one was open for 14% -> 4% of each run, Pallas kernels for 2% -> 3%
where the time goes in v2:
time: 402 us; the launch traced here: 397 us
  Pallas kernels  211 us (52%)
  matrix products  85.4 us (21%)
  waiting for transfers between devices  38.4 us (10%)
  local copies, waits for them, and re-layouts  36.1 us (9%)
  between operations  15.3 us (4%)
  blocking collectives  6.25 us (2%)
  other arithmetic  4.34 us (1%)
    pallas_call x1, Pallas kernels, closing(): pl.pallas_call(functools.partial(closing_kernel, model, maps), in_specs=[...  158 us
    all_gather x1, waiting for transfers between devices, per_device(): whole = lax.all_gather(normed, 'head', axis=0, tiled=True)  34.7 us
    dot_general x4, matrix products, t_mm(): lax.dot_general(a, b, (((0,), (0,)), ((), ())), preferred_element_type=F32)  32.4 us
    pallas_call x1, Pallas kernels, scan_bwd(): pl.pallas_call(functools.partial(bwd_kernel, span, heads, taps_n), grid=(...  31.7 us
    dot_general x4, matrix products, mm_t(): lax.dot_general(a, b, (((1,), (1,)), ((), ())), preferred_element_type=F32)  31.7 us
    dot_general x4, matrix products, mm(): return jnp.dot(a, b, preferred_element_type=F32)  21.4 us
    unnamed x84, local copies, waits for them, and re-layouts  19.4 us
    pallas_call x1, Pallas kernels, scan_fwd(): pl.pallas_call(functools.partial(fwd_kernel, span, heads, taps_n), grid=(...  12.4 us
  transfers between devices with their start and end apart: 2, of which 2 were waited for; matrix products, arithmetic and copies ran while one was open for 4% of the time, Pallas kernels for 3%

profile of v2, /device:TPU:0, one launch (start us, length us, event | category | flops | bytes accessed | tf_op | source)
XLA Modules:
  0.0 396.8 jit_solution(227922770211058847)
XLA Ops:
  7.3 1.6 fusion
  8.9 2.5 fusion.2
  11.5 0.7 all-gather.5.cloned.1.call-update
  12.2 0.3 copy.33
  14.1 34.7 %all-gather.3.cloned.1.call-done = bf16[1024,2048]{1,0:T(8,128)(2,1)} async-done(((bf16[256,2048]{1,0:T(8,128)(2,1)}), bf16[1024,2048]{1,0:T(8,128)(2,1)}) %all-gather.3.cloned.1.call-update) | async-done | bytes 4194320 | tf_op jit(solution)/shard_map/all_gather | solution.py:756
  48.8 4.7 %fusion.3.ss_ref.sh_ref = f32[1024,384]{1,0:T(8,128)S(1)} fusion(bf16[1024,2048]{1,0:T(8,128)(2,1)} %all-gather.3.cloned.1.call-done, bf16[2048,16]{1,0:T(8,128)(2,1)S(1)} %copy.33, bf16[2048,256]{1,0:T(8,128)(2,1)S(1)} %copy-done.17, bf16[384]{0:T(512)(128)(2,1)S(1)} %pad.24.clone), kind=kOutput, calls=%fused_computation.12 | convolution fusion | flops 1615331328 | bytes 6882048 | tf_op jit(solution)/shard_map/dot_general | solution.py:16
  53.6 4.5 %fusion.14.vp_ref.vh_ref = f32[1024,1024]{1,0:T(8,128)S(1)} fusion(bf16[1024,2048]{1,0:T(8,128)(2,1)S(1)} %copy-done.34, bf16[2048,1024]{1,0:T(8,128)(2,1)S(1)} %copy-done.29), kind=kOutput, calls=%fused_computation.42 | convolution fusion | flops 4294967296 | bytes 12582912 | tf_op jit(solution)/shard_map/dot_general | solution.py:16
  58.1 12.4 %scan_fwd.1 = (f32[1024,1024]{1,0:T(8,128)S(1)}, bf16[8,128,1024]{2,1,0:T(8,128)(2,1)S(1)}) custom-call(f32[1024,1024]{1,0:T(8,128)S(1)} %fusion.14.vp_ref.vh_ref, f32[1024,384]{1,0:T(8,128)S(1)} %fusion.3.ss_ref.sh_ref, f32[8,1024]{1,0:T(8,128)S(1)} %concatenate.13.cv_ref, f32[8,256]{1,0:T(8,128)S(1)} %maximum_maximum_fusion.3.cs_ref, ...), custom_call_target="tpu_custom_call" | custom-call | tf_op jit(solution)/shard_map/scan_fwd/pallas_call | solution.py:276
  70.5 2.0 copy-done
  72.6 2.0 copy-done.1
  74.5 1.3 copy-done.6
  75.8 6.1 %fusion.15.gate_ref = f32[1024,1024]{1,0:T(8,128)} fusion(bf16[1024,2048]{1,0:T(8,128)(2,1)S(1)} %copy-done.34, bf16[2048,1024]{1,0:T(8,128)(2,1)S(1)} %copy-done.31), kind=kOutput, calls=%fused_computation.43 | convolution fusion | flops 4294967296 | bytes 12582912 | tf_op jit(solution)/shard_map/dot_general | solution.py:16
  81.9 3.0 all-gather.5.cloned.1.call-done
  84.9 7.7 %fusion.16.dno_ref = f32[1024,1024]{1,0:T(8,128)S(1)} fusion(bf16[1024,2048]{1,0:T(8,128)(2,1)} %all-gather.5.cloned.1.call-done, bf16[1024,2048]{1,0:T(8,128)(2,1)} %param.31), kind=kOutput, calls=%fused_computation.44 | convolution fusion | flops 4294967296 | bytes 12582912 | tf_op jit(solution)/shard_map/dot_general | solution.py:20
  92.7 1.9 row_sums.1
  94.7 6.2 %psum.7 = f32[2,1024]{1,0:T(2,128)S(1)} all-reduce(f32[2,1024]{1,0:T(2,128)S(1)} %slice.64), channel_id=1, replica_groups=mesh['dp'=8,'head'=4] {'head'}, use_global_device_ids=true, to_apply=%region_1.2 | all-reduce | flops 2048 | bytes 16384 | tf_op jit(solution)/shard_map/psum | solution.py:773
  100.9 2.2 copy-done.3
  103.1 6.4 %norm_both.1 = (bf16[1024,1024]{1,0:T(8,128)(2,1)S(1)}, bf16[1024,1024]{1,0:T(8,128)(2,1)S(1)}, bf16[1024,1024]{1,0:T(8,128)(2,1)S(1)}, f32[8,1024]{1,0:T(8,128)S(1)}) custom-call(f32[1024,1024]{1,0:T(8,128)S(1)} %copy-done.3, f32[1024,1024]{1,0:T(8,128)} %fusion.15.gate_ref, f32[1024,1024]{1,0:T(8,128)} %copy-done.5, f32[8,1024]{1,0:T(8,128)S(1)} %concatenate.13.cv_ref, ...), custom_call_target="tpu_custom_call" | custom-call | tf_op jit(solution)/shard_map/norm_both/pallas_call | solution.py:419
  109.5 1.3 copy-done.7
  110.8 0.6 copy-done.8
  111.4 31.7 %scan_bwd.1 = (bf16[1024,1024]{1,0:T(8,128)(2,1)S(1)}, bf16[1024,384]{1,0:T(8,128)(2,1)S(1)}, f32[8,1024]{1,0:T(8,128)S(1)}, f32[8,256]{1,0:T(8,128)S(1)}, f32[8,128]{1,0:T(8,128)S(1)}) custom-call(f32[1024,1024]{1,0:T(8,128)} %copy-done, f32[1024,1024]{1,0:T(8,128)} %copy-done, f32[1024,384]{1,0:T(8,128)S(1)} %fusion.3.ss_ref.sh_ref, ...), custom_call_target="tpu_custom_call" | custom-call | tf_op jit(solution)/shard_map/scan_bwd/pallas_call | solution.py:311
  143.2 6.8 %fusion.18 = f32[1024,2048]{1,0:T(8,128)} fusion(bf16[1024,1024]{1,0:T(8,128)(2,1)S(1)} %get-tuple-element.40, bf16[2048,1024]{1,0:T(8,128)(2,1)S(1)} %copy-done.30), kind=kOutput, calls=%fused_computation.46 | convolution fusion | flops 4294967296 | bytes 14680064 | tf_op jit(solution)/shard_map/dot_general | solution.py:20
  150.1 6.8 %fusion.17 = f32[1024,2048]{1,0:T(8,128)} fusion(bf16[1024,1024]{1,0:T(8,128)(2,1)S(1)} %get-tuple-element.37, bf16[2048,1024]{1,0:T(8,128)(2,1)S(1)} %copy-done.32), kind=kOutput, calls=%fused_computation.45 | convolution fusion | flops 4294967296 | bytes 14680064 | tf_op jit(solution)/shard_map/dot_general | solution.py:20
  156.8 6.1 %convolution_convert_fusion = bf16[1024,2048]{1,0:T(8,128)(2,1)} fusion(bf16[1024,1024]{1,0:T(8,128)(2,1)S(1)} %get-tuple-element.36, bf16[1024,2048]{1,0:T(8,128)(2,1)S(1)} %copy-done.33), kind=kOutput, calls=%fused_computation.2 | convolution fusion | flops 4297064448 | bytes 10485760 | tf_op jit(solution)/shard_map/dot_general | solution.py:16
  162.9 16.2 %convert_bitcast_fusion = bf16[2048,1024]{0,1:T(8,128)(2,1)} fusion(bf16[1024,1024]{1,0:T(8,128)(2,1)S(1)} %get-tuple-element.36, bf16[1024,2048]{1,0:T(8,128)(2,1)S(1)} %copy-done.36), kind=kOutput, calls=%fused_computation.1 | convolution fusion | flops 4297064448 | bytes 10485760 | tf_op jit(solution)/shard_map/dot_general | solution.py:24
  179.1 6.5 %copy.34 = bf16[2048,1024]{1,0:T(8,128)(2,1)} copy(bf16[2048,1024]{0,1:T(8,128)(2,1)} %convert_bitcast_fusion) | data formatting | bytes 8388608 | tf_op jit(solution)/shard_map/convert_element_type | solution.py:776
  185.6 10.4 %add_convert_fusion = bf16[1024,2048]{1,0:T(8,128)(2,1)} fusion(f32[1024,2048]{1,0:T(8,128)} %fusion.17, f32[1024,2048]{1,0:T(8,128)} %fusion.18, bf16[1024,384]{1,0:T(8,128)(2,1)S(1)} %get-tuple-element.41, bf16[2048,16]{1,0:T(8,128)(2,1)S(1)} %copy.33, bf16[2048,256]{1,0:T(8,128)(2,1)S(1)} %copy-done.18, bf16[384]{0:T(512)(128)(2,1)S(1)} %pad.24.clone), kind=kOutput, calls=%fused_computation | convolution fusion | flops 1621622784 | bytes 22872832 | tf_op jit(solution)/shard_map/dot_general | solution.py:20
  196.0 6.3 %convolution_convert_fusion.1 = bf16[2048,1024]{1,0:T(8,128)(2,1)} fusion(bf16[1024,2048]{1,0:T(8,128)(2,1)S(1)} %copy-done.35, bf16[1024,1024]{1,0:T(8,128)(2,1)S(1)} %copy-done.15), kind=kOutput, calls=%fused_computation.3 | convolution fusion | flops 4297064448 | bytes 10485760 | tf_op jit(solution)/shard_map/dot_general | solution.py:24
  202.3 3.6 convolution_convert_fusion.3
  205.9 6.2 %convolution_convert_fusion.2 = bf16[2048,1024]{1,0:T(8,128)(2,1)} fusion(bf16[1024,2048]{1,0:T(8,128)(2,1)S(1)} %copy-done.35, bf16[1024,1024]{1,0:T(8,128)(2,1)S(1)} %copy-done.13), kind=kOutput, calls=%fused_computation.4 | convolution fusion | flops 4297064448 | bytes 10485760 | tf_op jit(solution)/shard_map/dot_general | solution.py:24
  212.2 158.4 %closing.1 = (bf16[256,2048]{1,0:T(8,128)(2,1)}, f32[256,2048]{1,0:T(8,128)}, f32[256,1024]{1,0:T(8,128)}, f32[256,1024]{1,0:T(8,128)}, f32[256,1024]{1,0:T(8,12...) custom-call(bf16[8,256,1024]{2,1,0:T(8,128)(2,1)} %bitcast.56, bf16[8,256,1024]{2,1,0:T(8,128)(2,1)} %bitcast.60, ...), custom_call_target="tpu_custom_call" | custom-call | tf_op jit(solution)/shard_map/closing/pallas_call | solution.py:722
  370.6 1.8 slice.51
  372.4 0.9 slice.52
  373.3 1.4 slice.53
  374.7 1.4 fusion.12
  376.1 0.8 fusion.13
  377.0 0.8 slice_reduce_fusion
  377.8 0.7 slice_reduce_fusion.1
  378.5 2.6 copy.36
  381.1 0.7 copy.35
  381.8 0.6 slice.65
  382.4 0.6 copy.39
  383.0 0.6 slice.56
  383.6 0.5 slice_bitcast_fusion.1
  384.1 2.4 copy.45
  386.5 1.3 copy.46
  387.8 1.0 copy.47
  388.8 1.0 copy.48
  (96 shorter events, 1.1 us)
Async XLA Ops:
  7.2 5.0 %copy-start.21 = (bf16[2048,16]{0,1:T(8,128)(2,1)S(1)}, bf16[2048,16]{0,1:T(8,128)(2,1)}, u32[]{:S(2)}) copy-start(bf16[2048,16]{0,1:T(8,128)(2,1)} %param.22) | copy-start | bytes 196612
  7.2 6.2 %copy-start.27 = (f32[16]{0:T(128)S(1)}, f32[16]{0:T(128)}, u32[]{:S(2)}) copy-start(f32[16]{0:T(128)} %param.29) | copy-start | bytes 196
  7.2 6.5 %copy-start.23 = (f32[1024]{0:T(1024)S(1)}, f32[1024]{0:T(1024)}, u32[]{:S(2)}) copy-start(f32[1024]{0:T(1024)} %param.24) | copy-start | bytes 12292
  7.2 6.5 %copy-start.24 = (f32[1024]{0:T(1024)S(1)}, f32[1024]{0:T(1024)}, u32[]{:S(2)}) copy-start(f32[1024]{0:T(1024)} %param.30) | copy-start | bytes 12292
  7.2 6.5 %copy-start.22 = (f32[4,1024]{1,0:T(4,128)S(1)}, f32[4,1024]{1,0:T(4,128)}, u32[]{:S(2)}) copy-start(f32[4,1024]{1,0:T(4,128)} %param.23) | copy-start | bytes 49156
  7.2 6.6 %copy-start.37 = (f32[16]{0:T(128)S(1)}, f32[16]{0:T(128)}, u32[]{:S(2)}) copy-start(f32[16]{0:T(128)} %param.28) | copy-start | bytes 196
  7.2 6.6 %copy-start.28 = (f32[16]{0:T(128)S(1)}, f32[16]{0:T(128)}, u32[]{:S(2)}) copy-start(f32[16]{0:T(128)} %param.27) | copy-start | bytes 196
  7.3 6.7 %copy-start.26 = (f32[256]{0:T(256)S(1)}, f32[256]{0:T(256)}, u32[]{:S(2)}) copy-start(f32[256]{0:T(256)} %param.26) | copy-start | bytes 3076
  7.3 6.7 %copy-start.25 = (f32[4,256]{1,0:T(4,128)S(1)}, f32[4,256]{1,0:T(4,128)}, u32[]{:S(2)}) copy-start(f32[4,256]{1,0:T(4,128)} %param.25) | copy-start | bytes 12292
  7.3 41.5 %copy-start.17 = (bf16[2048,256]{1,0:T(8,128)(2,1)S(1)}, bf16[2048,256]{1,0:T(8,128)(2,1)}, u32[]{:S(2)}) copy-start(bf16[2048,256]{1,0:T(8,128)(2,1)} %param.21) | copy-start | bytes 3145732
  7.3 41.5 %all-gather.3.cloned.1.call-start = ((), (), s32[]{:S(2)}) async-start(), calls=%async_computation | async-start | bytes 5242880 | tf_op jit(solution)/shard_map/all_gather | solution.py:756
  11.5 73.4 %all-gather.5.cloned.1.call-start = ((), (), s32[]{:S(2)}) async-start(), calls=%async_computation.1 | async-start | bytes 5242880 | tf_op jit(solution)/shard_map/all_gather | solution.py:757
  48.8 4.7 %copy-start.29 = (bf16[2048,1024]{1,0:T(8,128)(2,1)S(1)}, bf16[2048,1024]{1,0:T(8,128)(2,1)}, u32[]{:S(2)}) copy-start(bf16[2048,1024]{1,0:T(8,128)(2,1)} %param.20) | copy-start | bytes 12582916
  48.8 4.7 %copy-start.34 = (bf16[1024,2048]{1,0:T(8,128)(2,1)S(1)}, bf16[1024,2048]{1,0:T(8,128)(2,1)}, u32[]{:S(2)}) copy-start(bf16[1024,2048]{1,0:T(8,128)(2,1)} %all-gather.3.cloned.1.call-done) | copy-start | bytes 12582916
  58.1 17.7 %copy-start.31 = (bf16[2048,1024]{1,0:T(8,128)(2,1)S(1)}, bf16[2048,1024]{1,0:T(8,128)(2,1)}, u32[]{:S(2)}) copy-start(bf16[2048,1024]{1,0:T(8,128)(2,1)} %param.19) | copy-start | bytes 12582916
  70.5 2.0 copy-start
  72.6 2.0 copy-start.1
  74.5 1.3 copy-start.6
  84.9 7.7 %copy-start.2 = (f32[1024,1024]{1,0:T(8,128)S(1)}, f32[1024,1024]{1,0:T(8,128)}, u32[]{:S(2)}) copy-start(f32[1024,1024]{1,0:T(8,128)} %copy-done.1) | copy-start | bytes 12582916
  84.9 7.8 %copy-start.4 = (f32[1024,1024]{1,0:T(8,128)S(1)}, f32[1024,1024]{1,0:T(8,128)}, u32[]{:S(2)}) copy-start(f32[1024,1024]{1,0:T(8,128)} %fusion.15.gate_ref) | copy-start | bytes 12582916
  92.6 2.0 copy-start.5
  100.9 2.2 copy-start.3
  109.5 1.3 copy-start.7
  110.8 0.6 copy-start.8
  111.4 38.6 %copy-start.12 = (bf16[1024,1024]{1,0:T(8,128)(2,1)}, bf16[1024,1024]{1,0:T(8,128)(2,1)S(1)}, u32[]{:S(2)}) copy-start(bf16[1024,1024]{1,0:T(8,128)(2,1)S(1)} %get-tuple-element.37) | copy-start | bytes 6291460
  111.4 31.8 %copy-start.30 = (bf16[2048,1024]{1,0:T(8,128)(2,1)S(1)}, bf16[2048,1024]{1,0:T(8,128)(2,1)}, u32[]{:S(2)}) copy-start(bf16[2048,1024]{1,0:T(8,128)(2,1)} %param.20) | copy-start | bytes 12582916
  143.1 6.9 %copy-start.9 = (f32[8,1024]{1,0:T(8,128)}, f32[8,1024]{1,0:T(8,128)S(1)}, u32[]{:S(2)}) copy-start(f32[8,1024]{1,0:T(8,128)S(1)} %get-tuple-element.42.gcv_ref) | copy-start | bytes 98308
  143.1 6.9 %copy-start.10 = (f32[8,256]{1,0:T(8,128)}, f32[8,256]{1,0:T(8,128)S(1)}, u32[]{:S(2)}) copy-start(f32[8,256]{1,0:T(8,128)S(1)} %get-tuple-element.45.gcs_ref) | copy-start | bytes 24580
  143.2 6.9 %copy-start.11 = (f32[8,128]{1,0:T(8,128)}, f32[8,128]{1,0:T(8,128)S(1)}, u32[]{:S(2)}) copy-start(f32[8,128]{1,0:T(8,128)S(1)} %get-tuple-element.44.gh_ref) | copy-start | bytes 12292
  143.2 6.9 %copy-start.14 = (bf16[1024,1024]{1,0:T(8,128)(2,1)}, bf16[1024,1024]{1,0:T(8,128)(2,1)S(1)}, u32[]{:S(2)}) copy-start(bf16[1024,1024]{1,0:T(8,128)(2,1)S(1)} %get-tuple-element.40) | copy-start | bytes 6291460
  143.2 6.9 %copy-start.32 = (bf16[2048,1024]{1,0:T(8,128)(2,1)S(1)}, bf16[2048,1024]{1,0:T(8,128)(2,1)}, u32[]{:S(2)}) copy-start(bf16[2048,1024]{1,0:T(8,128)(2,1)} %param.19) | copy-start | bytes 12582916
  150.1 6.8 %copy-start.33 = (bf16[1024,2048]{1,0:T(8,128)(2,1)S(1)}, bf16[1024,2048]{1,0:T(8,128)(2,1)}, u32[]{:S(2)}) copy-start(bf16[1024,2048]{1,0:T(8,128)(2,1)} %param.31) | copy-start | bytes 12582916
  156.8 6.1 %copy-start.36 = (bf16[1024,2048]{1,0:T(8,128)(2,1)S(1)}, bf16[1024,2048]{1,0:T(8,128)(2,1)}, u32[]{:S(2)}) copy-start(bf16[1024,2048]{1,0:T(8,128)(2,1)} %all-gather.5.cloned.1.call-done) | copy-start | bytes 12582916
  179.1 6.5 %copy-start.18 = (bf16[2048,256]{1,0:T(8,128)(2,1)S(1)}, bf16[2048,256]{1,0:T(8,128)(2,1)}, u32[]{:S(2)}) copy-start(bf16[2048,256]{1,0:T(8,128)(2,1)} %param.21) | copy-start | bytes 3145732
  185.6 10.4 %copy-start.15 = (bf16[1024,1024]{1,0:T(8,128)(2,1)S(1)}, bf16[1024,1024]{1,0:T(8,128)(2,1)}, u32[]{:S(2)}) copy-start(bf16[1024,1024]{1,0:T(8,128)(2,1)} %copy-done.14) | copy-start | bytes 6291460
  185.6 10.4 %copy-start.35 = (bf16[1024,2048]{1,0:T(8,128)(2,1)S(1)}, bf16[1024,2048]{1,0:T(8,128)(2,1)}, u32[]{:S(2)}) copy-start(bf16[1024,2048]{1,0:T(8,128)(2,1)} %all-gather.3.cloned.1.call-done) | copy-start | bytes 12582916
  202.3 3.6 copy-start.13
  370.6 15.9 %copy-start.16 = (f32[256,2048]{1,0:T(8,128)S(1)}, f32[256,2048]{1,0:T(8,128)}, u32[]{:S(2)}) copy-start(f32[256,2048]{1,0:T(8,128)} %get-tuple-element.98) | copy-start | bytes 6291460
  378.5 9.3 %copy-start.20 = (f32[256,1024]{1,0:T(8,128)S(1)}, f32[256,1024]{1,0:T(8,128)}, u32[]{:S(2)}) copy-start(f32[256,1024]{1,0:T(8,128)} %get-tuple-element.100) | copy-start | bytes 3145732
  384.1 4.7 %copy-start.19 = (f32[256,1024]{1,0:T(8,128)S(1)}, f32[256,1024]{1,0:T(8,128)}, u32[]{:S(2)}) copy-start(f32[256,1024]{1,0:T(8,128)} %get-tuple-element.101) | copy-start | bytes 3145732
Sparse Core Ops, SparseCore 0:
  11.6 37.1 all-gather.2
  50.4 34.4 all-gather.4
